TPU v7x, 512 devices: a whole 4x8x8 slice. The times are simulated.
512 devices in a mesh: gx: 8 (over z_lo, core), gz: 16 (over y, z_hi), gy: 4 (over x).
Axes of the slice: x: 4, y: 8, z: 8 (z_hi: 2, z_lo: 4; z = z_hi * 4 + z_lo), core: 2. Of those that a mesh axis runs over, the one named last changes fastest.
Arguments:
- spectral: float32 [2, 512, 32, 2048], P(None, 'gz', 'gy', 'gx'), may hold values from -6 to 6
- shifts: int32 [512, 32], P('gz', 'gy'), may hold values from 0 to 2047
- colour: int32 [32, 2048], P('gy', 'gx'), may hold values 0 or 1
- pressure: float32 [512, 32, 2048], P('gz', 'gy', 'gx'), may hold values from -5 to 7
- source: float32 [512, 32, 2048], P('gz', 'gy', 'gx'), may hold values from -4.5 to 7
Outputs:
- log_perm: float32 [512, 32, 2048], P('gz', 'gy', 'gx')
- smoothed: float32 [512, 32, 2048], P('gz', 'gy', 'gx')
All inputs are finite; a program needn't handle non-finite values. No bound on the sum of `colour` on one device may be relied on, other than what follows from the above.
Results may differ from a plain program's by a relative error of at most 0.0038.
Values sent between devices are 32-bit elements; how exact they have to be, the bound alone decides.
A program may use at most 128 MiB of HBM per device.

v0:
```python
import functools
import math

import jax
import jax.numpy as jnp
import ml_dtypes
import numpy as np
from jax import lax
from jax.experimental import pallas as pl
from jax.experimental.pallas import tpu as pltpu
from jax.sharding import PartitionSpec as P

NX = 2048
STORE = 1.0
VERT = 65536.0
MESH = pl.DeviceIdType.MESH
GX = 8
GY = 4
GZ = 16
DEPTH = 32
ITEMS = 8
WIDTH = 256
ROWS = 32
F32 = jnp.float32
BF16 = jnp.bfloat16


def tables():
    j = np.arange(WIDTH)
    angle = 2.0 * np.pi * ((j[:, None] * j[None, :]) % WIDTH) / WIDTH
    dft = np.concatenate([np.cos(angle), -np.sin(angle)], axis=0) / math.sqrt(NX)
    high = dft.astype(ml_dtypes.bfloat16)
    low = (dft - high.astype(np.float64)).astype(ml_dtypes.bfloat16)
    dft_pair = np.stack([high, low])
    r = np.arange(GX)
    turn = 2.0 * np.pi * (r[:, None] * j[None, :]) / NX
    twiddle = np.stack([np.cos(turn), np.sin(turn)]).astype(np.float32)
    order = np.zeros((WIDTH, WIDTH), np.float32)
    for rr in range(8):
        for p in range(32):
            order[32 * rr + p, 8 * p + rr] = 1.0
    return dft_pair, twiddle, order.astype(ml_dtypes.bfloat16)


def cos_sin(turns):
    quadrant = (turns + 256) >> 9
    x = (turns - (quadrant << 9)).astype(F32) * (2.0 * math.pi / NX)
    x2 = x * x
    sine = x * (1.0 + x2 * (-1.0 / 6 + x2 * (1.0 / 120 + x2 * (-1.0 / 5040 + x2 * (1.0 / 362880)))))
    cosine = 1.0 + x2 * (-0.5 + x2 * (1.0 / 24 + x2 * (-1.0 / 720 + x2 * (1.0 / 40320))))
    swap = (quadrant & 1) == 1
    c = jnp.where(swap, sine, cosine)
    s = jnp.where(swap, cosine, sine)
    c = jnp.where(((quadrant + 1) & 2) == 2, -c, c)
    s = jnp.where((quadrant & 2) == 2, -s, s)
    return c, s


def dft4(z):
    (r0, i0), (r1, i1), (r2, i2), (r3, i3) = z
    ar, ai, br, bi = r0 + r2, i0 + i2, r0 - r2, i0 - i2
    cr, ci, dr, di = r1 + r3, i1 + i3, r1 - r3, i1 - i3
    return [(ar + cr, ai + ci), (br - di, bi + dr), (ar - cr, ai - ci), (br + di, bi - dr)]


def dft8(t):
    root = math.sqrt(0.5)
    even = [(t[k][0] + t[k + 4][0], t[k][1] + t[k + 4][1]) for k in range(4)]
    odd = [(t[k][0] - t[k + 4][0], t[k][1] - t[k + 4][1]) for k in range(4)]
    o1 = (root * (odd[1][0] - odd[1][1]), root * (odd[1][0] + odd[1][1]))
    o2 = (-odd[2][1], odd[2][0])
    o3 = (-root * (odd[3][0] + odd[3][1]), root * (odd[3][0] - odd[3][1]))
    ev = dft4(even)
    od = dft4([odd[0], o1, o2, o3])
    out = []
    for m in range(4):
        out += [ev[m], od[m]]
    return out


def split(value):
    high = value.astype(BF16)
    return high, (value - high.astype(F32)).astype(BF16)


def spectral_kernel(
    spec, shifts, dft_hbm, twiddle, order_hbm, out,
    xb, trig, lhs_hi, lhs_lo, zb, wb_hi, wb_lo, sb, dft, order,
    send1, recv1, send2, recv2, local,
):
    me = lax.axis_index("gx")
    barrier = pltpu.get_barrier_semaphore()

    def mine(slot):
        return pl.ds(4 * slot, 4)

    own = pltpu.make_async_copy(spec.at[:, mine(me)], xb.at[me], local.at[0])
    own.start()
    dft_copy = pltpu.make_async_copy(dft_hbm, dft, local.at[1])
    dft_copy.start()
    order_copy = pltpu.make_async_copy(order_hbm, order, local.at[2])
    order_copy.start()
    for i in range(1, GX):
        peer = lax.rem(me + i, GX)
        pl.semaphore_signal(barrier, inc=1, device_id={"gx": peer}, device_id_type=MESH)
    pl.semaphore_wait(barrier, GX - 1)

    def first(peer, slot, who):
        return pltpu.make_async_remote_copy(
            src_ref=spec.at[:, mine(peer)], dst_ref=xb.at[slot],
            send_sem=send1.at[peer], recv_sem=recv1.at[slot],
            device_id={"gx": who}, device_id_type=MESH,
        )

    for i in range(1, GX):
        peer = lax.rem(me + i, GX)
        first(peer, me, peer).start()

    lane = lax.broadcasted_iota(jnp.int32, (8, WIDTH), 1)
    lane1 = lax.broadcasted_iota(jnp.int32, (8, 128), 1)
    sub1 = lax.broadcasted_iota(jnp.int32, (8, 128), 0)
    for z in range(4):
        row = shifts[pl.ds(4 * me + z, 1), :].astype(F32)
        row = jnp.concatenate([row, jnp.zeros((1, 120), F32)], axis=1)
        row = jnp.where(lane1 == sub1, jnp.broadcast_to(row, (8, 128)), 0.0)
        shift = jnp.sum(row, axis=1, keepdims=True).astype(jnp.int32)
        shift = jnp.broadcast_to(shift, (8, WIDTH))

        def make_trig(d, carry, z=z, shift=shift):
            c, s = cos_sin((shift * (lane + d * WIDTH)) & (NX - 1))
            trig[0, d, pl.ds(8 * z, 8), :] = c
            trig[1, d, pl.ds(8 * z, 8), :] = s
            return carry

        lax.fori_loop(0, GX, make_trig, 0)

    own.wait()
    for i in range(1, GX):
        peer = lax.rem(me + GX - i, GX)
        first(peer, peer, peer).wait_recv()

    for zz in range(2):
        rows = pl.ds(16 * zz, 16)
        for h in range(2):
            cols = pl.ds(128 * h, 128)
            t = []
            for d in range(GX):
                xr = xb[d, 0, pl.ds(2 * zz, 2), :, cols].reshape(16, 128)
                xi = xb[d, 1, pl.ds(2 * zz, 2), :, cols].reshape(16, 128)
                c = trig[0, d, rows, cols]
                s = trig[1, d, rows, cols]
                t.append((xr * c - xi * s, xr * s + xi * c))
            y = dft8(t)
            for r in range(8):
                yr, yi = y[r]
                if r > 0:
                    c = twiddle[0, pl.ds(r, 1), cols]
                    s = twiddle[1, pl.ds(r, 1), cols]
                    yr, yi = yr * c - yi * s, yr * s + yi * c
                place = pl.ds(32 * r + 16 * zz, 16)
                hi, lo = split(yr)
                lhs_hi[place, pl.ds(128 * h, 128)] = hi
                lhs_lo[place, pl.ds(128 * h, 128)] = lo
                hi, lo = split(yi)
                lhs_hi[place, pl.ds(256 + 128 * h, 128)] = hi
                lhs_lo[place, pl.ds(256 + 128 * h, 128)] = lo

    dft_copy.wait()
    zb[...] = (
        jnp.dot(lhs_hi[...], dft[0], preferred_element_type=F32)
        + jnp.dot(lhs_hi[...], dft[1], preferred_element_type=F32)
        + jnp.dot(lhs_lo[...], dft[0], preferred_element_type=F32)
    )
    group = lax.broadcasted_iota(jnp.int32, (ROWS, 128), 1) // 32
    for e in range(8):
        column, g = e // 4, e % 4
        for h in range(2):
            total = None
            for rr in range(4):
                r = 4 * h + rr
                tile = zb[pl.ds(32 * r, 32), pl.ds(128 * column, 128)]
                turn = (32 * (rr - g)) % 128
                if turn:
                    tile = pltpu.roll(tile, turn, 1)
                total = tile if total is None else jnp.where(group == rr, tile, total)
            hi, lo = split(total)
            wb_hi[pl.ds(32 * e, 32), pl.ds(128 * h, 128)] = hi
            wb_lo[pl.ds(32 * e, 32), pl.ds(128 * h, 128)] = lo
    order_copy.wait()
    natural = jnp.dot(wb_hi[...], order[...], preferred_element_type=F32) + jnp.dot(
        wb_lo[...], order[...], preferred_element_type=F32
    )
    sb[...] = natural.reshape(8, 4, 8, WIDTH)

    def second(peer, slot, who):
        return pltpu.make_async_remote_copy(
            src_ref=sb.at[peer], dst_ref=out.at[mine(slot)],
            send_sem=send2.at[peer], recv_sem=recv2.at[slot],
            device_id={"gx": who}, device_id_type=MESH,
        )

    for i in range(1, GX):
        peer = lax.rem(me + i, GX)
        second(peer, me, peer).start()
    out[mine(me)] = sb[me]
    for i in range(1, GX):
        peer = lax.rem(me + GX - i, GX)
        second(peer, peer, peer).wait_recv()
    for i in range(1, GX):
        peer = lax.rem(me + i, GX)
        first(peer, me, peer).wait_send()
        second(peer, me, peer).wait_send()


def spectral_call(spectral, shifts):
    dft_pair, twiddle, order = tables()
    vmem = pl.BlockSpec(memory_space=pltpu.VMEM)
    anywhere = pl.BlockSpec(memory_space=pl.ANY)
    return pl.pallas_call(
        spectral_kernel,
        out_shape=jax.ShapeDtypeStruct((DEPTH, ITEMS, WIDTH), F32),
        in_specs=[anywhere, vmem, anywhere, vmem, anywhere],
        out_specs=vmem,
        scratch_shapes=[
            pltpu.VMEM((GX, 2, 4, 8, WIDTH), F32),
            pltpu.VMEM((2, GX, ROWS, WIDTH), F32),
            pltpu.VMEM((256, 512), BF16),
            pltpu.VMEM((256, 512), BF16),
            pltpu.VMEM((256, WIDTH), F32),
            pltpu.VMEM((256, WIDTH), BF16),
            pltpu.VMEM((256, WIDTH), BF16),
            pltpu.VMEM((GX, 4, 8, WIDTH), F32),
            pltpu.VMEM((2, 512, WIDTH), BF16),
            pltpu.VMEM((WIDTH, WIDTH), BF16),
            pltpu.SemaphoreType.DMA((GX,)),
            pltpu.SemaphoreType.DMA((GX,)),
            pltpu.SemaphoreType.DMA((GX,)),
            pltpu.SemaphoreType.DMA((GX,)),
            pltpu.SemaphoreType.DMA((3,)),
        ],
        compiler_params=pltpu.CompilerParams(
            collective_id=0, has_side_effects=True, vmem_limit_bytes=32 << 20
        ),
        name="spectral",
    )(spectral, shifts, jnp.asarray(dft_pair), jnp.asarray(twiddle), jnp.asarray(order))


def harmonic(center, beside):
    return 2.0 * center * beside / (center + beside)


LEVELS = (
    [(n, n - 1, n + 1) for n in range(1, 31, 2)],
    [(n, n - 2, min(n + 2, 31)) for n in range(2, 31, 4)],
    [(n, n - 4, min(n + 4, 31)) for n in range(4, 31, 8)],
    [(8, 0, 16), (24, 16, 31)],
    [(16, 0, 31)],
)


def sweep_kernel(
    log_perm, pressure, source, colour, out,
    perm, half, ww, we, ws, wn, dd, ff, cc, ll, rr, iv,
    xs1, xh1, ys1, yh1, zh, xs2, xh2, ys2, yh2,
    msg, got, ans, sol, msg2, got2, ans2, sol2,
    halo_send, halo_recv, gz_send, gz_recv,
):
    gx = lax.axis_index("gx")
    gy = lax.axis_index("gy")
    gz = lax.axis_index("gz")
    left, right = lax.rem(gx + GX - 1, GX), lax.rem(gx + 1, GX)
    south, north = lax.rem(gy + GY - 1, GY), lax.rem(gy + 1, GY)
    below, above = lax.rem(gz + GZ - 1, GZ), lax.rem(gz + 1, GZ)
    barrier = pltpu.get_barrier_semaphore()
    for who in ({"gx": left}, {"gx": right}, {"gy": south}, {"gy": north}):
        pl.semaphore_signal(barrier, inc=1, device_id=who, device_id_type=MESH)

    def greet(i, carry):
        peer = lax.rem(gz + i, GZ)
        pl.semaphore_signal(barrier, inc=1, device_id={"gz": peer}, device_id_type=MESH)
        return carry

    lax.fori_loop(1, GZ, greet, 0)

    lane1 = lax.broadcasted_iota(jnp.int32, (8, 128), 1)
    lane = lax.broadcasted_iota(jnp.int32, (8, WIDTH), 1)
    sub = lax.broadcasted_iota(jnp.int32, (8, WIDTH), 0)

    def pack(source_ref, slot, xs, ys):
        west = jnp.zeros((8, 128), F32)
        east = jnp.zeros((8, 128), F32)
        for z in range(DEPTH):
            tile = source_ref[z]
            west = jnp.where(lane1 == z, tile[:, 0:1], west)
            east = jnp.where(lane1 == z, tile[:, 255:256], east)
            ys[0, slot, pl.ds(z, 1), :] = tile[0:1, :]
            ys[1, slot, pl.ds(z, 1), :] = tile[7:8, :]
        xs[0, pl.ds(8 * slot, 8), :] = west
        xs[1, pl.ds(8 * slot, 8), :] = east

    def exchange(src, dst, index, who):
        return pltpu.make_async_remote_copy(
            src_ref=src, dst_ref=dst, send_sem=halo_send.at[index], recv_sem=halo_recv.at[index],
            device_id=who, device_id_type=MESH,
        )

    def make_perm(z, carry):
        perm[z] = jnp.exp(log_perm[z])
        return carry

    lax.fori_loop(0, DEPTH, make_perm, 0, unroll=4)
    pack(perm, 0, xs1, ys1)
    pack(pressure, 1, xs1, ys1)
    pl.semaphore_wait(barrier, 4 + GZ - 1)
    halos = [
        exchange(xs1.at[0], xh1.at[1], 0, {"gx": left}),
        exchange(xs1.at[1], xh1.at[0], 1, {"gx": right}),
        exchange(ys1.at[0], yh1.at[1], 2, {"gy": south}),
        exchange(ys1.at[1], yh1.at[0], 3, {"gy": north}),
        exchange(perm.at[0], zh.at[1], 4, {"gz": below}),
        exchange(perm.at[DEPTH - 1], zh.at[0], 5, {"gz": above}),
    ]
    for copy in halos:
        copy.start()
    for copy in halos:
        copy.wait_recv()

    west_open = (gx > 0).astype(F32)
    east_open = (gx < GX - 1).astype(F32)
    south_open = (gy > 0).astype(F32)
    north_open = (gy < GY - 1).astype(F32)

    def beside(value, west, east, lower, upper):
        vw = jnp.where(lane == 0, west, pltpu.roll(value, 1, 1))
        ve = jnp.where(lane == WIDTH - 1, east, pltpu.roll(value, WIDTH - 1, 1))
        vs = jnp.where(sub == 0, lower, pltpu.roll(value, 1, 0))
        vn = jnp.where(sub == 7, upper, pltpu.roll(value, 7, 0))
        return vw, ve, vs, vn

    def edges(z, xh, yh, slot):
        west = xh[0, pl.ds(8 * slot, 8), :][:, z:z + 1]
        east = xh[1, pl.ds(8 * slot, 8), :][:, z:z + 1]
        lower = yh[0, slot, pl.ds(z, 1), :]
        upper = yh[1, slot, pl.ds(z, 1), :]
        return west, east, lower, upper

    for z in range(DEPTH):
        p = perm[z]
        west, east, lower, upper = edges(z, xh1, yh1, 0)
        pw, pe, ps, pn = beside(
            p, west * west_open, east * east_open, lower * south_open, upper * north_open
        )
        aw, ae, as_, an = harmonic(p, pw), harmonic(p, pe), harmonic(p, ps), harmonic(p, pn)
        ww[z], we[z], ws[z], wn[z] = aw, ae, as_, an
        dd[z] = STORE + aw + ae + as_ + an
        vw, ve, vs, vn = beside(pressure[z], *edges(z, xh1, yh1, 1))
        ff[z] = source[z] + aw * vw + ae * ve + as_ * vs + an * vn
        if z < DEPTH - 1:
            cc[z] = VERT * harmonic(p, perm[z + 1])
    top_open = (gz < GZ - 1).astype(F32)
    w_top = VERT * harmonic(perm[DEPTH - 1], zh[1] * top_open)

    for level in LEVELS:
        for n, a, b in level:
            wl, wr, d, f = cc[a], cc[n], dd[n], ff[n]
            inv = 1.0 / (d + wl + wr)
            l, r = wl * inv, wr * inv
            ll[n], rr[n], iv[n] = l, r, inv
            cc[a] = l * wr
            dd[a] = dd[a] + l * d
            dd[b] = dd[b] + r * d
            ff[a] = ff[a] + l * f
            ff[b] = ff[b] + r * f

    def put(ref, kind, value):
        for h in range(2):
            ref[pl.ds(8 * h + kind, 8, stride=16), :] = value[:, 128 * h:128 * h + 128]

    def take(ref, kind):
        return jnp.concatenate(
            [ref[pl.ds(8 * h + kind, 8, stride=16), :] for h in range(2)], axis=1
        )

    def tile(index):
        return pl.ds(pl.multiple_of(8 * index, 8), 8)

    def everyone(src, dst, phase):
        def copy(peer, slot, who):
            return pltpu.make_async_remote_copy(
                src_ref=src.at[tile(peer)], dst_ref=dst.at[tile(slot)],
                send_sem=gz_send.at[phase, peer], recv_sem=gz_recv.at[phase, slot],
                device_id={"gz": who}, device_id_type=MESH,
            )

        def start(i, carry):
            peer = lax.rem(gz + i, GZ)
            copy(peer, gz, peer).start()
            return carry

        def finish(i, carry):
            peer = lax.rem(gz + GZ - i, GZ)
            copy(peer, peer, peer).wait_recv()
            return carry

        def drain(i, carry):
            peer = lax.rem(gz + i, GZ)
            copy(peer, gz, peer).wait_send()
            return carry

        lax.fori_loop(1, GZ, start, 0)
        dst[tile(gz), :] = src[tile(gz), :]
        lax.fori_loop(1, GZ, finish, 0)
        return lambda: lax.fori_loop(1, GZ, drain, 0)

    put(msg, 0, dd[0])
    put(msg, 1, dd[DEPTH - 1])
    put(msg, 2, cc[0])
    put(msg, 3, w_top)
    put(msg, 4, ff[0])
    put(msg, 5, ff[DEPTH - 1])
    drains = [everyone(msg, got, 0)]

    def kind(ref, k):
        return ref[pl.ds(k, GZ, stride=8), :]

    d0, d1, c, w = kind(got, 0), kind(got, 1), kind(got, 2), kind(got, 3)
    f0, f1 = kind(got, 4), kind(got, 5)
    last_inv = 1.0 / (d1 + c + w)
    last_l, last_r = c * last_inv, w * last_inv

    def up(value, step):
        return pltpu.roll(value, step, 0)

    def down(value, step):
        return pltpu.roll(value, GZ - step, 0)

    e = d0 + last_l * d1 + up(last_r * d1, 1)
    b = last_l * w
    a = up(b, 1)
    alphas = []
    for step in (1, 2, 4, 8):
        inv = 1.0 / (e + a + b)
        alpha, beta = a * up(inv, step), b * down(inv, step)
        alphas.append((step, alpha, beta))
        e = e + alpha * up(e, step) + beta * down(e, step)
        if step < 8:
            a, b = alpha * up(a, step), beta * down(b, step)
    final_inv = 1.0 / e

    def reduced(f0, f1, ans):
        f = f0 + last_l * f1 + up(last_r * f1, 1)
        for step, alpha, beta in alphas:
            f = f + alpha * up(f, step) + beta * down(f, step)
        first = f * final_inv
        last = f1 * last_inv + last_l * first + last_r * down(first, 1)
        ans[pl.ds(0, GZ, stride=8), :] = first
        ans[pl.ds(1, GZ, stride=8), :] = last

    msg2[...] = jnp.zeros_like(msg2)
    ans[...] = jnp.zeros_like(ans)
    ans2[...] = jnp.zeros_like(ans2)
    reduced(f0, f1, ans)
    drains.append(everyone(ans, sol, 1))

    def substitute(sol, merge):
        u = {0: take(sol, 0), DEPTH - 1: take(sol, 1)}
        merge(0, u[0])
        merge(DEPTH - 1, u[DEPTH - 1])
        for level in reversed(LEVELS):
            for n, a, b in level:
                u[n] = ff[n] * iv[n] + ll[n] * u[a] + rr[n] * u[b]
                merge(n, u[n])

    tint = colour[...]

    def merge_half(z, u):
        half[z] = jnp.where(tint == 0, u, pressure[z])

    substitute(sol, merge_half)
    pack(half, 0, xs2, ys2)
    halos2 = [
        exchange(xs2.at[0], xh2.at[1], 6, {"gx": left}),
        exchange(xs2.at[1], xh2.at[0], 7, {"gx": right}),
        exchange(ys2.at[0], yh2.at[1], 8, {"gy": south}),
        exchange(ys2.at[1], yh2.at[0], 9, {"gy": north}),
    ]
    for copy in halos2:
        copy.start()
    for copy in halos2:
        copy.wait_recv()
    for z in range(DEPTH):
        vw, ve, vs, vn = beside(half[z], *edges(z, xh2, yh2, 0))
        ff[z] = source[z] + ww[z] * vw + we[z] * ve + ws[z] * vs + wn[z] * vn
    for level in LEVELS:
        for n, a, b in level:
            f = ff[n]
            ff[a] = ff[a] + ll[n] * f
            ff[b] = ff[b] + rr[n] * f
    put(msg2, 0, ff[0])
    put(msg2, 1, ff[DEPTH - 1])
    drains.append(everyone(msg2, got2, 2))
    reduced(kind(got2, 0), kind(got2, 1), ans2)
    drains.append(everyone(ans2, sol2, 3))

    def merge_out(z, u):
        out[z] = jnp.where(tint == 1, u, half[z])

    substitute(sol2, merge_out)
    for copy in halos + halos2:
        copy.wait_send()
    for drain in drains:
        drain()


def sweep_call(log_perm, pressure, source, colour):
    vmem = pl.BlockSpec(memory_space=pltpu.VMEM)
    field = pltpu.VMEM((DEPTH, ITEMS, WIDTH), F32)
    board = pltpu.VMEM((8 * GZ, 128), F32)
    return pl.pallas_call(
        sweep_kernel,
        out_shape=jax.ShapeDtypeStruct((DEPTH, ITEMS, WIDTH), F32),
        in_specs=[vmem] * 4,
        out_specs=vmem,
        scratch_shapes=[field] * 12
        + [
            pltpu.VMEM((2, 16, 128), F32),
            pltpu.VMEM((2, 16, 128), F32),
            pltpu.VMEM((2, 2, DEPTH, WIDTH), F32),
            pltpu.VMEM((2, 2, DEPTH, WIDTH), F32),
            pltpu.VMEM((2, ITEMS, WIDTH), F32),
            pltpu.VMEM((2, 8, 128), F32),
            pltpu.VMEM((2, 8, 128), F32),
            pltpu.VMEM((2, 1, DEPTH, WIDTH), F32),
            pltpu.VMEM((2, 1, DEPTH, WIDTH), F32),
        ]
        + [board] * 8
        + [
            pltpu.SemaphoreType.DMA((10,)),
            pltpu.SemaphoreType.DMA((10,)),
            pltpu.SemaphoreType.DMA((4, GZ)),
            pltpu.SemaphoreType.DMA((4, GZ)),
        ],
        compiler_params=pltpu.CompilerParams(
            collective_id=1, has_side_effects=True, vmem_limit_bytes=32 << 20
        ),
        name="sweep",
    )(log_perm, pressure, source, colour)


def body(spectral, shifts, colour, pressure, source):
    log_perm = spectral_call(spectral, shifts)
    smoothed = sweep_call(log_perm, pressure, source, colour)
    return (log_perm, smoothed)


def solution(mesh):
    in_specs = (
        P(None, "gz", "gy", "gx"),
        P("gz", "gy"),
        P("gy", "gx"),
        P("gz", "gy", "gx"),
        P("gz", "gy", "gx"),
    )
    out_specs = (P("gz", "gy", "gx"), P("gz", "gy", "gx"))
    return jax.shard_map(body, mesh=mesh, in_specs=in_specs, out_specs=out_specs, check_vma=False)
```

profile of v0, /device:TPU:1, one launch (start us, length us, event | category | flops | bytes accessed | tf_op | source)
XLA Modules:
  0.0 85.1 jit_solution(13075152888086167262)
XLA Ops:
  0.6 0.0 copy-start.5
  0.6 0.8 copy.10.shifts
  1.4 0.0 copy-done.5
  1.4 0.0 copy-start
  1.4 1.0 %copy-done = f32[2,32,8,256]{3,2,1,0:T(8,128)S(1)} copy-done((f32[2,32,8,256]{3,2,1,0:T(8,128)S(1)}, f32[2,32,8,256]{3,2,1,0:T(8,128)}, u32[]{:S(2)}) %copy-start) | copy-done | bytes 524312
  2.5 0.0 copy-start.1
  2.5 1.0 %copy-done.1 = bf16[2,512,256]{2,1,0:T(8,128)(2,1)S(1)} copy-done((bf16[2,512,256]{2,1,0:T(8,128)(2,1)S(1)}, bf16[2,512,256]{2,1,0:T(8,128)(2,1)}, u32[]{:S(2)}) %copy-start.1) | copy-done | bytes 524312
  3.5 0.0 copy-start.4
  3.5 0.9 %copy-done.4 = bf16[256,256]{1,0:T(8,128)(2,1)S(1)} copy-done((bf16[256,256]{1,0:T(8,128)(2,1)S(1)}, bf16[256,256]{1,0:T(8,128)(2,1)}, u32[]{:S(2)}) %copy-start.4) | copy-done | bytes 131096
  4.4 0.0 copy-start.2
  4.4 0.0 copy-start.3
  4.4 0.0 copy-start.6
  4.4 28.1 %spectral.1.log_perm = f32[32,8,256]{2,1,0:T(8,128)S(1)} custom-call(f32[2,32,8,256]{3,2,1,0:T(8,128)S(1)} %copy-done, s32[32,8]{1,0:T(8,128)S(1)} %copy.10.shifts, bf16[2,512,256]{2,1,0:T(8,128)(2,1)S(1)} %copy-done.1, f32[2,8,256]{2,1,0:T(8,128)S(1)} %copy-done.5, bf16[256,256]{1,0:T(8,128)(2,1)S(1)} %copy-done.4), custom_call_target="tpu_custom_call" | custom-call | tf_op jit(solution)/shard_map/spectral/pallas_call | solution.py:219
  32.5 0.0 copy-done.2
  32.5 0.0 copy-done.3
  32.5 0.0 copy-done.6
  32.5 51.2 %sweep.1 = f32[32,8,256]{2,1,0:T(8,128)S(1)} custom-call(f32[32,8,256]{2,1,0:T(8,128)S(1)} %spectral.1.log_perm, f32[32,8,256]{2,1,0:T(8,128)S(1)} %copy-done.2, f32[32,8,256]{2,1,0:T(8,128)S(1)} %copy-done.3, s32[8,256]{1,0:T(8,128)S(1)} %copy-done.6), custom_call_target="tpu_custom_call" | custom-call | tf_op jit(solution)/shard_map/sweep/pallas_call | solution.py:519
  83.7 0.7 copy.13
  84.4 0.7 copy.14
Async XLA Ops:
  0.6 0.8 copy-start.5
  1.4 1.0 %copy-start = (f32[2,32,8,256]{3,2,1,0:T(8,128)S(1)}, f32[2,32,8,256]{3,2,1,0:T(8,128)}, u32[]{:S(2)}) copy-start(f32[2,32,8,256]{3,2,1,0:T(8,128)} %spec.1) | copy-start | bytes 1572868
  2.5 1.0 %copy-start.1 = (bf16[2,512,256]{2,1,0:T(8,128)(2,1)S(1)}, bf16[2,512,256]{2,1,0:T(8,128)(2,1)}, u32[]{:S(2)}) copy-start(bf16[2,512,256]{2,1,0:T(8,128)(2,1)} %constant.6.clone.dft_hbm) | copy-start | bytes 1572868
  3.5 0.9 %copy-start.4 = (bf16[256,256]{1,0:T(8,128)(2,1)S(1)}, bf16[256,256]{1,0:T(8,128)(2,1)}, u32[]{:S(2)}) copy-start(bf16[256,256]{1,0:T(8,128)(2,1)} %constant.8.clone.order_hbm) | copy-start | bytes 393220
  4.4 28.1 %copy-start.2 = (f32[32,8,256]{2,1,0:T(8,128)S(1)}, f32[32,8,256]{2,1,0:T(8,128)}, u32[]{:S(2)}) copy-start(f32[32,8,256]{2,1,0:T(8,128)} %pressure.1) | copy-start | bytes 786436
  4.4 28.1 %copy-start.3 = (f32[32,8,256]{2,1,0:T(8,128)S(1)}, f32[32,8,256]{2,1,0:T(8,128)}, u32[]{:S(2)}) copy-start(f32[32,8,256]{2,1,0:T(8,128)} %source.1) | copy-start | bytes 786436
  4.4 28.1 %copy-start.6 = (s32[8,256]{1,0:T(8,128)S(1)}, s32[8,256]{1,0:T(8,128)}, u32[]{:S(2)}) copy-start(s32[8,256]{1,0:T(8,128)} %colour.1) | copy-start | bytes 24580
where the time goes:
time: 86 us; the launch traced here: 85.1 us
  Pallas kernels  79.3 us (92%)
  local copies, waits for them, and re-layouts  5.18 us (6%)
    pallas_call x1, Pallas kernels, sweep_call(): pl.pallas_call(sweep_kernel, out_shape=jax.ShapeDtypeStruct((DEPTH, ITEMS...  51.2 us
    pallas_call x1, Pallas kernels, spectral_call(): pl.pallas_call(spectral_kernel, out_shape=jax.ShapeDtypeStruct((DEPTH, IT...  28.1 us
    unnamed x17, local copies, waits for them, and re-layouts  5.18 us

commit v1 on v0

--- a/solution.py
+++ b/solution.py
@@ -83,13 +83,12 @@
     return high, (value - high.astype(F32)).astype(BF16)
 
 
-def spectral_kernel(
-    spec, shifts, dft_hbm, twiddle, order_hbm, out,
-    xb, trig, lhs_hi, lhs_lo, zb, wb_hi, wb_lo, sb, dft, order,
-    send1, recv1, send2, recv2, local,
+def spectral_part(
+    spec, shifts, dft_hbm, twiddle_hbm, order_hbm, out,
+    xb, trig, lhs_hi, lhs_lo, zb, wb_hi, wb_lo, sb, dft, twiddle, order,
+    send1, recv1, send2, recv2, local, greet_all, meanwhile,
 ):
     me = lax.axis_index("gx")
-    barrier = pltpu.get_barrier_semaphore()
 
     def mine(slot):
         return pl.ds(4 * slot, 4)
@@ -100,10 +99,9 @@
     dft_copy.start()
     order_copy = pltpu.make_async_copy(order_hbm, order, local.at[2])
     order_copy.start()
-    for i in range(1, GX):
-        peer = lax.rem(me + i, GX)
-        pl.semaphore_signal(barrier, inc=1, device_id={"gx": peer}, device_id_type=MESH)
-    pl.semaphore_wait(barrier, GX - 1)
+    twiddle_copy = pltpu.make_async_copy(twiddle_hbm, twiddle, local.at[3])
+    twiddle_copy.start()
+    greet_all()
 
     def first(peer, slot, who):
         return pltpu.make_async_remote_copy(
@@ -115,14 +113,12 @@
     for i in range(1, GX):
         peer = lax.rem(me + i, GX)
         first(peer, me, peer).start()
+    meanwhile()
 
     lane = lax.broadcasted_iota(jnp.int32, (8, WIDTH), 1)
-    lane1 = lax.broadcasted_iota(jnp.int32, (8, 128), 1)
-    sub1 = lax.broadcasted_iota(jnp.int32, (8, 128), 0)
+    lane0 = lax.broadcasted_iota(jnp.int32, (ITEMS, DEPTH), 1)
     for z in range(4):
-        row = shifts[pl.ds(4 * me + z, 1), :].astype(F32)
-        row = jnp.concatenate([row, jnp.zeros((1, 120), F32)], axis=1)
-        row = jnp.where(lane1 == sub1, jnp.broadcast_to(row, (8, 128)), 0.0)
+        row = jnp.where(lane0 == 4 * me + z, shifts[...].astype(F32), 0.0)
         shift = jnp.sum(row, axis=1, keepdims=True).astype(jnp.int32)
         shift = jnp.broadcast_to(shift, (8, WIDTH))
 
@@ -139,6 +135,7 @@
         peer = lax.rem(me + GX - i, GX)
         first(peer, peer, peer).wait_recv()
 
+    twiddle_copy.wait()
     for zz in range(2):
         rows = pl.ds(16 * zz, 16)
         for h in range(2):
@@ -206,43 +203,14 @@
     for i in range(1, GX):
         peer = lax.rem(me + GX - i, GX)
         second(peer, peer, peer).wait_recv()
-    for i in range(1, GX):
-        peer = lax.rem(me + i, GX)
-        first(peer, me, peer).wait_send()
-        second(peer, me, peer).wait_send()
-
-
-def spectral_call(spectral, shifts):
-    dft_pair, twiddle, order = tables()
-    vmem = pl.BlockSpec(memory_space=pltpu.VMEM)
-    anywhere = pl.BlockSpec(memory_space=pl.ANY)
-    return pl.pallas_call(
-        spectral_kernel,
-        out_shape=jax.ShapeDtypeStruct((DEPTH, ITEMS, WIDTH), F32),
-        in_specs=[anywhere, vmem, anywhere, vmem, anywhere],
-        out_specs=vmem,
-        scratch_shapes=[
-            pltpu.VMEM((GX, 2, 4, 8, WIDTH), F32),
-            pltpu.VMEM((2, GX, ROWS, WIDTH), F32),
-            pltpu.VMEM((256, 512), BF16),
-            pltpu.VMEM((256, 512), BF16),
-            pltpu.VMEM((256, WIDTH), F32),
-            pltpu.VMEM((256, WIDTH), BF16),
-            pltpu.VMEM((256, WIDTH), BF16),
-            pltpu.VMEM((GX, 4, 8, WIDTH), F32),
-            pltpu.VMEM((2, 512, WIDTH), BF16),
-            pltpu.VMEM((WIDTH, WIDTH), BF16),
-            pltpu.SemaphoreType.DMA((GX,)),
-            pltpu.SemaphoreType.DMA((GX,)),
-            pltpu.SemaphoreType.DMA((GX,)),
-            pltpu.SemaphoreType.DMA((GX,)),
-            pltpu.SemaphoreType.DMA((3,)),
-        ],
-        compiler_params=pltpu.CompilerParams(
-            collective_id=0, has_side_effects=True, vmem_limit_bytes=32 << 20
-        ),
-        name="spectral",
-    )(spectral, shifts, jnp.asarray(dft_pair), jnp.asarray(twiddle), jnp.asarray(order))
+
+    def drain():
+        for i in range(1, GX):
+            peer = lax.rem(me + i, GX)
+            first(peer, me, peer).wait_send()
+            second(peer, me, peer).wait_send()
+
+    return drain
 
 
 def harmonic(center, beside):
@@ -258,77 +226,127 @@
 )
 
 
-def sweep_kernel(
-    log_perm, pressure, source, colour, out,
-    perm, half, ww, we, ws, wn, dd, ff, cc, ll, rr, iv,
-    xs1, xh1, ys1, yh1, zh, xs2, xh2, ys2, yh2,
-    msg, got, ans, sol, msg2, got2, ans2, sol2,
-    halo_send, halo_recv, gz_send, gz_recv,
+def field_kernel(
+    spec, shifts, dft_hbm, twiddle_hbm, order_hbm, pressure_hbm, source_hbm, colour_hbm,
+    log_perm, out, *scratch,
 ):
+    (
+        xb, trig, lhs_hi, lhs_lo, zb, wb_hi, wb_lo, sb, dft, twiddle, order,
+        send1, recv1, send2, recv2, local,
+        pressure, source, colour,
+        perm, half, ww, we, ws, wn, dd, ff, cc, ll, rr, iv,
+        xs0, xh0, ys0, yh0, xs1, xh1, ys1, yh1, xs2, xh2, ys2, yh2,
+        msg, got, ans, sol, msg2, got2, ans2, sol2,
+        halo_send, halo_recv, gz_send, gz_recv,
+    ) = scratch
     gx = lax.axis_index("gx")
     gy = lax.axis_index("gy")
     gz = lax.axis_index("gz")
     left, right = lax.rem(gx + GX - 1, GX), lax.rem(gx + 1, GX)
     south, north = lax.rem(gy + GY - 1, GY), lax.rem(gy + 1, GY)
-    below, above = lax.rem(gz + GZ - 1, GZ), lax.rem(gz + 1, GZ)
-    barrier = pltpu.get_barrier_semaphore()
-    for who in ({"gx": left}, {"gx": right}, {"gy": south}, {"gy": north}):
-        pl.semaphore_signal(barrier, inc=1, device_id=who, device_id_type=MESH)
-
-    def greet(i, carry):
-        peer = lax.rem(gz + i, GZ)
-        pl.semaphore_signal(barrier, inc=1, device_id={"gz": peer}, device_id_type=MESH)
-        return carry
-
-    lax.fori_loop(1, GZ, greet, 0)
+    drains = []
+
+    pressure_copy = pltpu.make_async_copy(pressure_hbm, pressure, local.at[4])
+    source_copy = pltpu.make_async_copy(source_hbm, source, local.at[5])
+    colour_copy = pltpu.make_async_copy(colour_hbm, colour, local.at[6])
+
+    def greet_all():
+        barrier = pltpu.get_barrier_semaphore()
+
+        def greet(i, carry):
+            peer = lax.rem(gz + i, GZ)
+            pl.semaphore_signal(barrier, inc=1, device_id={"gz": peer}, device_id_type=MESH)
+            return carry
+
+        lax.fori_loop(1, GZ, greet, 0)
+        for i in range(1, GX):
+            peer = lax.rem(gx + i, GX)
+            pl.semaphore_signal(barrier, inc=1, device_id={"gx": peer}, device_id_type=MESH)
+        for who in (south, north):
+            pl.semaphore_signal(barrier, inc=1, device_id={"gy": who}, device_id_type=MESH)
+        pressure_copy.start()
+        source_copy.start()
+        colour_copy.start()
+        pl.semaphore_wait(barrier, GX - 1 + GZ - 1 + 2)
 
     lane1 = lax.broadcasted_iota(jnp.int32, (8, 128), 1)
     lane = lax.broadcasted_iota(jnp.int32, (8, WIDTH), 1)
     sub = lax.broadcasted_iota(jnp.int32, (8, WIDTH), 0)
 
-    def pack(source_ref, slot, xs, ys):
+    def pack(source_ref, xs, ys):
         west = jnp.zeros((8, 128), F32)
         east = jnp.zeros((8, 128), F32)
         for z in range(DEPTH):
             tile = source_ref[z]
             west = jnp.where(lane1 == z, tile[:, 0:1], west)
             east = jnp.where(lane1 == z, tile[:, 255:256], east)
-            ys[0, slot, pl.ds(z, 1), :] = tile[0:1, :]
-            ys[1, slot, pl.ds(z, 1), :] = tile[7:8, :]
-        xs[0, pl.ds(8 * slot, 8), :] = west
-        xs[1, pl.ds(8 * slot, 8), :] = east
-
-    def exchange(src, dst, index, who):
-        return pltpu.make_async_remote_copy(
-            src_ref=src, dst_ref=dst, send_sem=halo_send.at[index], recv_sem=halo_recv.at[index],
-            device_id=who, device_id_type=MESH,
+            ys[0, pl.ds(z, 1), :] = tile[0:1, :]
+            ys[1, pl.ds(z, 1), :] = tile[7:8, :]
+        xs[0] = west
+        xs[1] = east
+
+    sides = (
+        (0, 1, {"gx": left}, gx > 0, gx < GX - 1),
+        (1, 0, {"gx": right}, gx < GX - 1, gx > 0),
+        (0, 1, {"gy": south}, gy > 0, gy < GY - 1),
+        (1, 0, {"gy": north}, gy < GY - 1, gy > 0),
+    )
+
+    def halo(phase, xs, xh, ys, yh):
+        def copy(k):
+            src, dst = (xs, xh) if k < 2 else (ys, yh)
+            side, there, who, _, _ = sides[k]
+            return pltpu.make_async_remote_copy(
+                src_ref=src.at[side], dst_ref=dst.at[there],
+                send_sem=halo_send.at[phase, k], recv_sem=halo_recv.at[phase, k],
+                device_id=who, device_id_type=MESH,
+            )
+
+        def each(which, action):
+            for k in range(4):
+                pl.when(sides[k][which])(functools.partial(action, k))
+
+        def blank(k):
+            dst = xh if k < 2 else yh
+            there = sides[k][1]
+
+            def fill():
+                dst[there] = jnp.zeros(dst.shape[1:], F32)
+
+            pl.when(jnp.logical_not(sides[k][4]))(fill)
+
+        each(3, lambda k: copy(k).start())
+        for k in range(4):
+            blank(k)
+        drains.append(lambda: each(3, lambda k: copy(k).wait_send()))
+        return lambda: each(4, lambda k: copy(k).wait_recv())
+
+    arrived = []
+
+    def meanwhile():
+        pressure_copy.wait()
+        pack(pressure, xs0, ys0)
+        arrived.append(halo(0, xs0, xh0, ys0, yh0))
+
+    drains.append(
+        spectral_part(
+            spec, shifts, dft_hbm, twiddle_hbm, order_hbm, log_perm,
+            xb, trig, lhs_hi, lhs_lo, zb, wb_hi, wb_lo, sb, dft, twiddle, order,
+            send1, recv1, send2, recv2, local, greet_all, meanwhile,
         )
+    )
 
     def make_perm(z, carry):
         perm[z] = jnp.exp(log_perm[z])
         return carry
 
     lax.fori_loop(0, DEPTH, make_perm, 0, unroll=4)
-    pack(perm, 0, xs1, ys1)
-    pack(pressure, 1, xs1, ys1)
-    pl.semaphore_wait(barrier, 4 + GZ - 1)
-    halos = [
-        exchange(xs1.at[0], xh1.at[1], 0, {"gx": left}),
-        exchange(xs1.at[1], xh1.at[0], 1, {"gx": right}),
-        exchange(ys1.at[0], yh1.at[1], 2, {"gy": south}),
-        exchange(ys1.at[1], yh1.at[0], 3, {"gy": north}),
-        exchange(perm.at[0], zh.at[1], 4, {"gz": below}),
-        exchange(perm.at[DEPTH - 1], zh.at[0], 5, {"gz": above}),
-    ]
-    for copy in halos:
-        copy.start()
-    for copy in halos:
-        copy.wait_recv()
-
-    west_open = (gx > 0).astype(F32)
-    east_open = (gx < GX - 1).astype(F32)
-    south_open = (gy > 0).astype(F32)
-    north_open = (gy < GY - 1).astype(F32)
+    pack(perm, xs1, ys1)
+    wait_perm = halo(1, xs1, xh1, ys1, yh1)
+    source_copy.wait()
+    colour_copy.wait()
+    arrived[0]()
+    wait_perm()
 
     def beside(value, west, east, lower, upper):
         vw = jnp.where(lane == 0, west, pltpu.roll(value, 1, 1))
@@ -337,28 +355,23 @@
         vn = jnp.where(sub == 7, upper, pltpu.roll(value, 7, 0))
         return vw, ve, vs, vn
 
-    def edges(z, xh, yh, slot):
-        west = xh[0, pl.ds(8 * slot, 8), :][:, z:z + 1]
-        east = xh[1, pl.ds(8 * slot, 8), :][:, z:z + 1]
-        lower = yh[0, slot, pl.ds(z, 1), :]
-        upper = yh[1, slot, pl.ds(z, 1), :]
+    def edges(z, xh, yh):
+        west = xh[0][:, z:z + 1]
+        east = xh[1][:, z:z + 1]
+        lower = yh[0, pl.ds(z, 1), :]
+        upper = yh[1, pl.ds(z, 1), :]
         return west, east, lower, upper
 
     for z in range(DEPTH):
         p = perm[z]
-        west, east, lower, upper = edges(z, xh1, yh1, 0)
-        pw, pe, ps, pn = beside(
-            p, west * west_open, east * east_open, lower * south_open, upper * north_open
-        )
+        pw, pe, ps, pn = beside(p, *edges(z, xh1, yh1))
         aw, ae, as_, an = harmonic(p, pw), harmonic(p, pe), harmonic(p, ps), harmonic(p, pn)
         ww[z], we[z], ws[z], wn[z] = aw, ae, as_, an
         dd[z] = STORE + aw + ae + as_ + an
-        vw, ve, vs, vn = beside(pressure[z], *edges(z, xh1, yh1, 1))
+        vw, ve, vs, vn = beside(pressure[z], *edges(z, xh0, yh0))
         ff[z] = source[z] + aw * vw + ae * ve + as_ * vs + an * vn
         if z < DEPTH - 1:
             cc[z] = VERT * harmonic(p, perm[z + 1])
-    top_open = (gz < GZ - 1).astype(F32)
-    w_top = VERT * harmonic(perm[DEPTH - 1], zh[1] * top_open)
 
     for level in LEVELS:
         for n, a, b in level:
@@ -415,16 +428,20 @@
     put(msg, 0, dd[0])
     put(msg, 1, dd[DEPTH - 1])
     put(msg, 2, cc[0])
-    put(msg, 3, w_top)
-    put(msg, 4, ff[0])
-    put(msg, 5, ff[DEPTH - 1])
-    drains = [everyone(msg, got, 0)]
+    put(msg, 3, perm[0])
+    put(msg, 4, perm[DEPTH - 1])
+    put(msg, 5, ff[0])
+    put(msg, 6, ff[DEPTH - 1])
+    put(msg, 7, ff[0])
+    drains.append(everyone(msg, got, 0))
 
     def kind(ref, k):
         return ref[pl.ds(k, GZ, stride=8), :]
 
-    d0, d1, c, w = kind(got, 0), kind(got, 1), kind(got, 2), kind(got, 3)
-    f0, f1 = kind(got, 4), kind(got, 5)
+    d0, d1, c, p0, p1 = (kind(got, k) for k in range(5))
+    f0, f1 = kind(got, 5), kind(got, 6)
+    segment = lax.broadcasted_iota(jnp.int32, (GZ, 128), 0)
+    w = jnp.where(segment < GZ - 1, VERT * harmonic(p1, pltpu.roll(p0, GZ - 1, 0)), 0.0)
     last_inv = 1.0 / (d1 + c + w)
     last_l, last_r = c * last_inv, w * last_inv
 
@@ -477,19 +494,10 @@
         half[z] = jnp.where(tint == 0, u, pressure[z])
 
     substitute(sol, merge_half)
-    pack(half, 0, xs2, ys2)
-    halos2 = [
-        exchange(xs2.at[0], xh2.at[1], 6, {"gx": left}),
-        exchange(xs2.at[1], xh2.at[0], 7, {"gx": right}),
-        exchange(ys2.at[0], yh2.at[1], 8, {"gy": south}),
-        exchange(ys2.at[1], yh2.at[0], 9, {"gy": north}),
-    ]
-    for copy in halos2:
-        copy.start()
-    for copy in halos2:
-        copy.wait_recv()
+    pack(half, xs2, ys2)
+    halo(2, xs2, xh2, ys2, yh2)()
     for z in range(DEPTH):
-        vw, ve, vs, vn = beside(half[z], *edges(z, xh2, yh2, 0))
+        vw, ve, vs, vn = beside(half[z], *edges(z, xh2, yh2))
         ff[z] = source[z] + ww[z] * vw + we[z] * ve + ws[z] * vs + wn[z] * vn
     for level in LEVELS:
         for n, a, b in level:
@@ -506,50 +514,56 @@
         out[z] = jnp.where(tint == 1, u, half[z])
 
     substitute(sol2, merge_out)
-    for copy in halos + halos2:
-        copy.wait_send()
     for drain in drains:
         drain()
 
 
-def sweep_call(log_perm, pressure, source, colour):
+def field_call(spectral, shifts, colour, pressure, source):
+    dft_pair, twiddle, order = tables()
     vmem = pl.BlockSpec(memory_space=pltpu.VMEM)
-    field = pltpu.VMEM((DEPTH, ITEMS, WIDTH), F32)
+    hbm = pl.BlockSpec(memory_space=pltpu.HBM)
+    block = (DEPTH, ITEMS, WIDTH)
+    field = pltpu.VMEM(block, F32)
     board = pltpu.VMEM((8 * GZ, 128), F32)
+    columns = pltpu.VMEM((2, ITEMS, 128), F32)
+    rows = pltpu.VMEM((2, DEPTH, WIDTH), F32)
+    dma = pltpu.SemaphoreType.DMA
     return pl.pallas_call(
-        sweep_kernel,
-        out_shape=jax.ShapeDtypeStruct((DEPTH, ITEMS, WIDTH), F32),
-        in_specs=[vmem] * 4,
-        out_specs=vmem,
-        scratch_shapes=[field] * 12
-        + [
-            pltpu.VMEM((2, 16, 128), F32),
-            pltpu.VMEM((2, 16, 128), F32),
-            pltpu.VMEM((2, 2, DEPTH, WIDTH), F32),
-            pltpu.VMEM((2, 2, DEPTH, WIDTH), F32),
-            pltpu.VMEM((2, ITEMS, WIDTH), F32),
-            pltpu.VMEM((2, 8, 128), F32),
-            pltpu.VMEM((2, 8, 128), F32),
-            pltpu.VMEM((2, 1, DEPTH, WIDTH), F32),
-            pltpu.VMEM((2, 1, DEPTH, WIDTH), F32),
+        field_kernel,
+        out_shape=[jax.ShapeDtypeStruct(block, F32)] * 2,
+        in_specs=[hbm, vmem] + [hbm] * 6,
+        out_specs=[vmem, vmem],
+        scratch_shapes=[
+            pltpu.VMEM((GX, 2, 4, 8, WIDTH), F32),
+            pltpu.VMEM((2, GX, ROWS, WIDTH), F32),
+            pltpu.VMEM((256, 512), BF16),
+            pltpu.VMEM((256, 512), BF16),
+            pltpu.VMEM((256, WIDTH), F32),
+            pltpu.VMEM((256, WIDTH), BF16),
+            pltpu.VMEM((256, WIDTH), BF16),
+            pltpu.VMEM((GX, 4, 8, WIDTH), F32),
+            pltpu.VMEM((2, 512, WIDTH), BF16),
+            pltpu.VMEM((2, GX, WIDTH), F32),
+            pltpu.VMEM((WIDTH, WIDTH), BF16),
+            dma((GX,)), dma((GX,)), dma((GX,)), dma((GX,)), dma((7,)),
+            field, field, pltpu.VMEM((ITEMS, WIDTH), jnp.int32),
         ]
+        + [field] * 12
+        + [columns, columns, rows, rows] * 3
         + [board] * 8
-        + [
-            pltpu.SemaphoreType.DMA((10,)),
-            pltpu.SemaphoreType.DMA((10,)),
-            pltpu.SemaphoreType.DMA((4, GZ)),
-            pltpu.SemaphoreType.DMA((4, GZ)),
-        ],
+        + [dma((3, 4)), dma((3, 4)), dma((4, GZ)), dma((4, GZ))],
         compiler_params=pltpu.CompilerParams(
-            collective_id=1, has_side_effects=True, vmem_limit_bytes=32 << 20
+            collective_id=0, has_side_effects=True, vmem_limit_bytes=32 << 20
         ),
-        name="sweep",
-    )(log_perm, pressure, source, colour)
+        name="field",
+    )(
+        spectral, shifts.T, jnp.asarray(dft_pair), jnp.asarray(twiddle), jnp.asarray(order),
+        pressure, source, colour,
+    )
 
 
 def body(spectral, shifts, colour, pressure, source):
-    log_perm = spectral_call(spectral, shifts)
-    smoothed = sweep_call(log_perm, pressure, source, colour)
+    log_perm, smoothed = field_call(spectral, shifts, colour, pressure, source)
     return (log_perm, smoothed)
 
 

time: 86 us -> 85 us (0.988)
  Pallas kernels: 79.3 us -> 74.8 us
  local copies, waits for them, and re-layouts: 5.18 us -> 8.39 us
    pallas_call x2 -> x1, Pallas kernels: 79.3 us -> 74.8 us  [field_call(): pl.pallas_call(field_kernel, out_shape=[jax.ShapeDtypeStruct(block, F32)]...]
    unnamed x17 -> x18, local copies, waits for them, and re-layouts: 5.18 us -> 8.39 us
where the time goes in v1:
time: 85 us; the launch traced here: 83.8 us
  Pallas kernels  74.8 us (88%)
  local copies, waits for them, and re-layouts  8.39 us (10%)
    pallas_call x1, Pallas kernels, field_call(): pl.pallas_call(field_kernel, out_shape=[jax.ShapeDtypeStruct(block, F32)]...  74.8 us
    unnamed x18, local copies, waits for them, and re-layouts  8.39 us

profile of v1, /device:TPU:1, one launch (start us, length us, event | category | flops | bytes accessed | tf_op | source)
XLA Modules:
  0.0 83.8 jit_solution(11609001363981230546)
XLA Ops:
  0.6 0.0 copy-start
  0.6 1.0 %copy-done = f32[2,32,8,256]{3,2,1,0:T(8,128)S(1)} copy-done((f32[2,32,8,256]{3,2,1,0:T(8,128)S(1)}, f32[2,32,8,256]{3,2,1,0:T(8,128)}, u32[]{:S(2)}) %copy-start) | copy-done | bytes 524312
  1.7 0.0 copy-start.1
  1.7 1.0 %copy-done.1 = bf16[2,512,256]{2,1,0:T(8,128)(2,1)S(1)} copy-done((bf16[2,512,256]{2,1,0:T(8,128)(2,1)S(1)}, bf16[2,512,256]{2,1,0:T(8,128)(2,1)}, u32[]{:S(2)}) %copy-start.1) | copy-done | bytes 524312
  2.7 0.0 copy-start.2
  2.7 0.9 %copy-done.2 = f32[32,8,256]{2,1,0:T(8,128)S(1)} copy-done((f32[32,8,256]{2,1,0:T(8,128)S(1)}, f32[32,8,256]{2,1,0:T(8,128)}, u32[]{:S(2)}) %copy-start.2) | copy-done | bytes 262168
  3.7 0.0 copy-start.3
  3.7 0.9 %copy-done.3 = f32[32,8,256]{2,1,0:T(8,128)S(1)} copy-done((f32[32,8,256]{2,1,0:T(8,128)S(1)}, f32[32,8,256]{2,1,0:T(8,128)}, u32[]{:S(2)}) %copy-start.3) | copy-done | bytes 262168
  4.6 0.0 copy-start.4
  4.6 0.9 %copy-done.4 = bf16[256,256]{1,0:T(8,128)(2,1)S(1)} copy-done((bf16[256,256]{1,0:T(8,128)(2,1)S(1)}, bf16[256,256]{1,0:T(8,128)(2,1)}, u32[]{:S(2)}) %copy-start.4) | copy-done | bytes 131096
  5.5 0.0 copy-start.5
  5.5 0.7 copy-done.5
  6.2 0.0 copy-start.6
  6.2 0.7 copy-done.6
  6.9 0.0 copy-start.7
  6.9 0.7 copy-done.7
  7.6 74.8 %field.1 = (f32[32,8,256]{2,1,0:T(8,128)S(1)}, f32[32,8,256]{2,1,0:T(8,128)S(1)}) custom-call(f32[2,32,8,256]{3,2,1,0:T(8,128)S(1)} %copy-done, s32[8,32]{1,0:T(8,128)S(1)} %bitcast.1, bf16[2,512,256]{2,1,0:T(8,128)(2,1)S(1)} %copy-done.1, f32[2,8,256]{2,1,0:T(8,128)S(1)} %copy-done.5, bf16[256,256]{1,0:T(8,128)(2,1)S(1)} %copy-done.4, ...), custom_call_target="tpu_custom_call" | custom-call | tf_op jit(solution)/shard_map/field/pallas_call | solution.py:531
  82.4 0.7 copy.12
  83.1 0.7 copy.13
Async XLA Ops:
  0.6 1.0 %copy-start = (f32[2,32,8,256]{3,2,1,0:T(8,128)S(1)}, f32[2,32,8,256]{3,2,1,0:T(8,128)}, u32[]{:S(2)}) copy-start(f32[2,32,8,256]{3,2,1,0:T(8,128)} %spec.1) | copy-start | bytes 1572868
  1.7 1.0 %copy-start.1 = (bf16[2,512,256]{2,1,0:T(8,128)(2,1)S(1)}, bf16[2,512,256]{2,1,0:T(8,128)(2,1)}, u32[]{:S(2)}) copy-start(bf16[2,512,256]{2,1,0:T(8,128)(2,1)} %constant.6.clone.dft_hbm) | copy-start | bytes 1572868
  2.7 0.9 %copy-start.2 = (f32[32,8,256]{2,1,0:T(8,128)S(1)}, f32[32,8,256]{2,1,0:T(8,128)}, u32[]{:S(2)}) copy-start(f32[32,8,256]{2,1,0:T(8,128)} %pressure_hbm.1) | copy-start | bytes 786436
  3.7 0.9 %copy-start.3 = (f32[32,8,256]{2,1,0:T(8,128)S(1)}, f32[32,8,256]{2,1,0:T(8,128)}, u32[]{:S(2)}) copy-start(f32[32,8,256]{2,1,0:T(8,128)} %source_hbm.1) | copy-start | bytes 786436
  4.6 0.9 %copy-start.4 = (bf16[256,256]{1,0:T(8,128)(2,1)S(1)}, bf16[256,256]{1,0:T(8,128)(2,1)}, u32[]{:S(2)}) copy-start(bf16[256,256]{1,0:T(8,128)(2,1)} %constant.8.clone.order_hbm) | copy-start | bytes 393220
  5.5 0.7 copy-start.5
  6.2 0.7 copy-start.6
  6.9 0.7 copy-start.7

commit v2 on v1

--- a/solution.py
+++ b/solution.py
@@ -228,12 +228,12 @@
 
 def field_kernel(
     spec, shifts, dft_hbm, twiddle_hbm, order_hbm, pressure_hbm, source_hbm, colour_hbm,
-    log_perm, out, *scratch,
+    log_perm_hbm, out, *scratch,
 ):
     (
         xb, trig, lhs_hi, lhs_lo, zb, wb_hi, wb_lo, sb, dft, twiddle, order,
         send1, recv1, send2, recv2, local,
-        pressure, source, colour,
+        pressure, source, colour, log_perm,
         perm, half, ww, we, ws, wn, dd, ff, cc, ll, rr, iv,
         xs0, xh0, ys0, yh0, xs1, xh1, ys1, yh1, xs2, xh2, ys2, yh2,
         msg, got, ans, sol, msg2, got2, ans2, sol2,
@@ -340,6 +340,9 @@
         perm[z] = jnp.exp(log_perm[z])
         return carry
 
+    log_perm_copy = pltpu.make_async_copy(log_perm, log_perm_hbm, local.at[7])
+    log_perm_copy.start()
+    drains.append(log_perm_copy.wait)
     lax.fori_loop(0, DEPTH, make_perm, 0, unroll=4)
     pack(perm, xs1, ys1)
     wait_perm = halo(1, xs1, xh1, ys1, yh1)
@@ -532,7 +535,7 @@
         field_kernel,
         out_shape=[jax.ShapeDtypeStruct(block, F32)] * 2,
         in_specs=[hbm, vmem] + [hbm] * 6,
-        out_specs=[vmem, vmem],
+        out_specs=[hbm, vmem],
         scratch_shapes=[
             pltpu.VMEM((GX, 2, 4, 8, WIDTH), F32),
             pltpu.VMEM((2, GX, ROWS, WIDTH), F32),
@@ -545,15 +548,15 @@
             pltpu.VMEM((2, 512, WIDTH), BF16),
             pltpu.VMEM((2, GX, WIDTH), F32),
             pltpu.VMEM((WIDTH, WIDTH), BF16),
-            dma((GX,)), dma((GX,)), dma((GX,)), dma((GX,)), dma((7,)),
-            field, field, pltpu.VMEM((ITEMS, WIDTH), jnp.int32),
+            dma((GX,)), dma((GX,)), dma((GX,)), dma((GX,)), dma((8,)),
+            field, field, pltpu.VMEM((ITEMS, WIDTH), jnp.int32), field,
         ]
         + [field] * 12
         + [columns, columns, rows, rows] * 3
         + [board] * 8
         + [dma((3, 4)), dma((3, 4)), dma((4, GZ)), dma((4, GZ))],
         compiler_params=pltpu.CompilerParams(
-            collective_id=0, has_side_effects=True, vmem_limit_bytes=32 << 20
+            collective_id=0, has_side_effects=True, vmem_limit_bytes=56 << 20
         ),
         name="field",
     )(

time: 85 us -> 79.8 us (0.939)
  local copies, waits for them, and re-layouts: 8.39 us -> 2.42 us
    unnamed x18 -> x4, local copies, waits for them, and re-layouts: 8.39 us -> 2.42 us
where the time goes in v2:
time: 79.8 us; the launch traced here: 78.4 us
  Pallas kernels  75.3 us (94%)
  local copies, waits for them, and re-layouts  2.42 us (3%)
    pallas_call x1, Pallas kernels, field_call(): pl.pallas_call(field_kernel, out_shape=[jax.ShapeDtypeStruct(block, F32)]...  75.3 us
    unnamed x4, local copies, waits for them, and re-layouts  2.42 us

profile of v2, /device:TPU:1, one launch (start us, length us, event | category | flops | bytes accessed | tf_op | source)
XLA Modules:
  0.0 78.4 jit_solution(12043046902436157434)
XLA Ops:
  0.6 75.3 %field.1 = (f32[32,8,256]{2,1,0:T(8,128)}, f32[32,8,256]{2,1,0:T(8,128)}) custom-call(f32[2,32,8,256]{3,2,1,0:T(8,128)} %spec.1, s32[8,32]{1,0:T(8,128)} %bitcast.1, bf16[2,512,256]{2,1,0:T(8,128)(2,1)} %constant.6.clone.dft_hbm, f32[2,8,256]{2,1,0:T(8,128)} %constant.7.clone.twiddle_hbm, bf16[256,256]{1,0:T(8,128)(2,1)} %constant.8.clone.order_hbm, ...), custom_call_target="tpu_custom_call" | custom-call | tf_op jit(solution)/shard_map/field/pallas_call | solution.py:534
  75.9 0.0 copy-start
  76.0 1.7 %copy.12 = f32[32,8,256]{2,1,0:T(8,128)} copy(f32[32,8,256]{2,1,0:T(8,128)} %get-tuple-element.4) | data formatting | bytes 524288
  77.7 0.0 copy-done
  77.7 0.7 copy.13
Async XLA Ops:
  75.9 1.7 %copy-start = (f32[32,8,256]{2,1,0:T(8,128)S(1)}, f32[32,8,256]{2,1,0:T(8,128)}, u32[]{:S(2)}) copy-start(f32[32,8,256]{2,1,0:T(8,128)} %get-tuple-element.5) | copy-start | bytes 786436

commit v3 on v1

--- a/solution.py
+++ b/solution.py
@@ -227,16 +227,16 @@
 
 
 def field_kernel(
-    spec, shifts, dft_hbm, twiddle_hbm, order_hbm, pressure_hbm, source_hbm, colour_hbm,
+    spec, shifts_hbm, dft_hbm, twiddle_hbm, order_hbm, pressure_hbm, source_hbm, colour_hbm,
     log_perm, out, *scratch,
 ):
     (
         xb, trig, lhs_hi, lhs_lo, zb, wb_hi, wb_lo, sb, dft, twiddle, order,
         send1, recv1, send2, recv2, local,
-        pressure, source, colour,
+        pressure, source, colour, shifts,
         perm, half, ww, we, ws, wn, dd, ff, cc, ll, rr, iv,
         xs0, xh0, ys0, yh0, xs1, xh1, ys1, yh1, xs2, xh2, ys2, yh2,
-        msg, got, ans, sol, msg2, got2, ans2, sol2,
+        msg, got, ans, sol, gains, taken, chain, sums, others,
         halo_send, halo_recv, gz_send, gz_recv,
     ) = scratch
     gx = lax.axis_index("gx")
@@ -248,6 +248,7 @@
 
     pressure_copy = pltpu.make_async_copy(pressure_hbm, pressure, local.at[4])
     source_copy = pltpu.make_async_copy(source_hbm, source, local.at[5])
+    shifts_copy = pltpu.make_async_copy(shifts_hbm, shifts, local.at[7])
     colour_copy = pltpu.make_async_copy(colour_hbm, colour, local.at[6])
 
     def greet_all():
@@ -264,6 +265,7 @@
             pl.semaphore_signal(barrier, inc=1, device_id={"gx": peer}, device_id_type=MESH)
         for who in (south, north):
             pl.semaphore_signal(barrier, inc=1, device_id={"gy": who}, device_id_type=MESH)
+        shifts_copy.start()
         pressure_copy.start()
         source_copy.start()
         colour_copy.start()
@@ -327,6 +329,7 @@
         pressure_copy.wait()
         pack(pressure, xs0, ys0)
         arrived.append(halo(0, xs0, xh0, ys0, yh0))
+        shifts_copy.wait()
 
     drains.append(
         spectral_part(
@@ -394,36 +397,36 @@
             [ref[pl.ds(8 * h + kind, 8, stride=16), :] for h in range(2)], axis=1
         )
 
-    def tile(index):
-        return pl.ds(pl.multiple_of(8 * index, 8), 8)
-
-    def everyone(src, dst, phase):
-        def copy(peer, slot, who):
+    def everyone(src, dst, phase, size):
+        def tile(index):
+            return pl.ds(pl.multiple_of(size * index, 8), size)
+
+        def copy(peer, slot):
             return pltpu.make_async_remote_copy(
                 src_ref=src.at[tile(peer)], dst_ref=dst.at[tile(slot)],
                 send_sem=gz_send.at[phase, peer], recv_sem=gz_recv.at[phase, slot],
-                device_id={"gz": who}, device_id_type=MESH,
+                device_id={"gz": peer}, device_id_type=MESH,
             )
 
         def start(i, carry):
             peer = lax.rem(gz + i, GZ)
-            copy(peer, gz, peer).start()
+            copy(peer, gz).start()
             return carry
 
         def finish(i, carry):
             peer = lax.rem(gz + GZ - i, GZ)
-            copy(peer, peer, peer).wait_recv()
+            copy(peer, peer).wait_recv()
             return carry
 
         def drain(i, carry):
             peer = lax.rem(gz + i, GZ)
-            copy(peer, gz, peer).wait_send()
+            copy(peer, gz).wait_send()
             return carry
 
         lax.fori_loop(1, GZ, start, 0)
         dst[tile(gz), :] = src[tile(gz), :]
-        lax.fori_loop(1, GZ, finish, 0)
-        return lambda: lax.fori_loop(1, GZ, drain, 0)
+        drains.append(lambda: lax.fori_loop(1, GZ, drain, 0))
+        return lambda: lax.fori_loop(1, GZ, finish, 0)
 
     put(msg, 0, dd[0])
     put(msg, 1, dd[DEPTH - 1])
@@ -433,7 +436,7 @@
     put(msg, 5, ff[0])
     put(msg, 6, ff[DEPTH - 1])
     put(msg, 7, ff[0])
-    drains.append(everyone(msg, got, 0))
+    everyone(msg, got, 0, 8)()
 
     def kind(ref, k):
         return ref[pl.ds(k, GZ, stride=8), :]
@@ -454,33 +457,61 @@
     e = d0 + last_l * d1 + up(last_r * d1, 1)
     b = last_l * w
     a = up(b, 1)
-    alphas = []
+    f = f0 + last_l * f1 + up(last_r * f1, 1)
     for step in (1, 2, 4, 8):
         inv = 1.0 / (e + a + b)
         alpha, beta = a * up(inv, step), b * down(inv, step)
-        alphas.append((step, alpha, beta))
         e = e + alpha * up(e, step) + beta * down(e, step)
+        f = f + alpha * up(f, step) + beta * down(f, step)
         if step < 8:
             a, b = alpha * up(a, step), beta * down(b, step)
-    final_inv = 1.0 / e
-
-    def reduced(f0, f1, ans):
-        f = f0 + last_l * f1 + up(last_r * f1, 1)
-        for step, alpha, beta in alphas:
-            f = f + alpha * up(f, step) + beta * down(f, step)
-        first = f * final_inv
-        last = f1 * last_inv + last_l * first + last_r * down(first, 1)
-        ans[pl.ds(0, GZ, stride=8), :] = first
-        ans[pl.ds(1, GZ, stride=8), :] = last
-
-    msg2[...] = jnp.zeros_like(msg2)
+    first = f / e
     ans[...] = jnp.zeros_like(ans)
-    ans2[...] = jnp.zeros_like(ans2)
-    reduced(f0, f1, ans)
-    drains.append(everyone(ans, sol, 1))
-
-    def substitute(sol, merge):
-        u = {0: take(sol, 0), DEPTH - 1: take(sol, 1)}
+    ans[pl.ds(0, GZ, stride=8), :] = first
+    ans[pl.ds(1, GZ, stride=8), :] = (
+        f1 * last_inv + last_l * first + last_r * down(first, 1)
+    )
+    wait_sol = everyone(ans, sol, 1, 8)
+
+    links = [jnp.zeros((1, 128), F32)] * 2
+    for i in range(GZ):
+        j = GZ - 1 - i
+        eb, et = links
+        at_i, at_j = pl.ds(i, 1), pl.ds(j, 1)
+        chain[2, at_i, :] = eb
+        chain[5, at_j, :] = et
+        low = d0[i:i + 1] + eb
+        rho = c[i:i + 1] / (low + c[i:i + 1])
+        low = d1[i:i + 1] + rho * low
+        tau = w[i:i + 1] / (low + w[i:i + 1])
+        chain[0, at_i, :] = rho
+        chain[1, at_i, :] = tau
+        high = d1[j:j + 1] + et
+        sigma = c[j:j + 1] / (high + c[j:j + 1])
+        high = d0[j:j + 1] + sigma * high
+        chain[3, at_j, :] = sigma
+        if j > 0:
+            upsilon = w[j - 1:j] / (high + w[j - 1:j])
+            chain[4, pl.ds(j - 1, 1), :] = upsilon
+        links = [tau * low, upsilon * high]
+    chain[4, pl.ds(GZ - 1, 1), :] = jnp.zeros((1, 128), F32)
+    tau, upsilon = chain[1], chain[4]
+    climb = up(tau * chain[0], 1)
+    descend = upsilon * down(chain[3], 1)
+    from_below, from_above = [None, up(tau, 1)], [None, upsilon]
+    for k in range(2, GZ):
+        from_below.append(climb * up(from_below[-1], 1))
+        from_above.append(descend * down(from_above[-1], 1))
+    gains[...] = jnp.zeros_like(gains)
+    for k in range(1, GZ):
+        gains[pl.ds(k, GZ, stride=24), :] = from_below[k] + from_above[GZ - k]
+    gains[pl.ds(GZ, GZ, stride=24), :] = chain[2]
+    gains[pl.ds(GZ + 1, GZ, stride=24), :] = chain[5]
+    wait_gains = everyone(gains, taken, 2, 24)
+    wait_sol()
+
+    def substitute(first, last, merge):
+        u = {0: first, DEPTH - 1: last}
         merge(0, u[0])
         merge(DEPTH - 1, u[DEPTH - 1])
         for level in reversed(LEVELS):
@@ -493,9 +524,24 @@
     def merge_half(z, u):
         half[z] = jnp.where(tint == 0, u, pressure[z])
 
-    substitute(sol, merge_half)
+    substitute(take(sol, 0), take(sol, 1), merge_half)
     pack(half, xs2, ys2)
-    halo(2, xs2, xh2, ys2, yh2)()
+    wait_half = halo(2, xs2, xh2, ys2, yh2)
+
+    def gain(k):
+        return jnp.concatenate(
+            [taken[pl.ds(24 * h + k, 8, stride=48), :] for h in range(2)], axis=1
+        )
+
+    wait_gains()
+    c = cc[0]
+    low = dd[0] + gain(GZ)
+    high = dd[DEPTH - 1] + gain(GZ + 1)
+    low_inv = 1.0 / (low + c)
+    rho = c * low_inv
+    sigma = c / (high + c)
+    high_inv = 1.0 / (high + rho * low)
+    wait_half()
     for z in range(DEPTH):
         vw, ve, vs, vn = beside(half[z], *edges(z, xh2, yh2))
         ff[z] = source[z] + ww[z] * vw + we[z] * ve + ws[z] * vs + wn[z] * vn
@@ -504,22 +550,61 @@
             f = ff[n]
             ff[a] = ff[a] + ll[n] * f
             ff[b] = ff[b] + rr[n] * f
-    put(msg2, 0, ff[0])
-    put(msg2, 1, ff[DEPTH - 1])
-    drains.append(everyone(msg2, got2, 2))
-    reduced(kind(got2, 0), kind(got2, 1), ans2)
-    drains.append(everyone(ans2, sol2, 3))
+    f0, f1 = ff[0], ff[DEPTH - 1]
+    sums[0] = f1 + rho * f0
+    sums[1] = f0 + sigma * f1
+
+    def cast(i):
+        peer = lax.rem(gz + i, GZ)
+        return pltpu.make_async_remote_copy(
+            src_ref=sums.at[lax.div(gz + i, GZ)], dst_ref=others.at[gz],
+            send_sem=gz_send.at[3, peer], recv_sem=gz_recv.at[3, gz],
+            device_id={"gz": peer}, device_id_type=MESH,
+        )
+
+    def heard(i):
+        peer = lax.rem(gz + GZ - i, GZ)
+        return pltpu.make_async_remote_copy(
+            src_ref=sums.at[0], dst_ref=others.at[peer],
+            send_sem=gz_send.at[3, peer], recv_sem=gz_recv.at[3, peer],
+            device_id={"gz": peer}, device_id_type=MESH,
+        )
+
+    def start_cast(i, carry):
+        cast(i).start()
+        return carry
+
+    def drain_cast(i, carry):
+        cast(i).wait_send()
+        return carry
+
+    def wait_heard(i, carry):
+        heard(i).wait_recv()
+        return carry
+
+    lax.fori_loop(1, GZ, start_cast, 0)
+    drains.append(lambda: lax.fori_loop(1, GZ, drain_cast, 0))
+    lax.fori_loop(1, GZ, wait_heard, 0)
+    for i in range(1, GZ):
+        part = gain(i) * others[lax.rem(gz + GZ - i, GZ)]
+        f0 = f0 + jnp.where(gz >= i, part, 0.0)
+        f1 = f1 + jnp.where(gz >= i, 0.0, part)
+    last = (f1 + rho * f0) * high_inv
+    first = f0 * low_inv + rho * last
 
     def merge_out(z, u):
         out[z] = jnp.where(tint == 1, u, half[z])
 
-    substitute(sol2, merge_out)
+    substitute(first, last, merge_out)
     for drain in drains:
         drain()
 
 
+def pin(value):
+    return pltpu.with_memory_space_constraint(value, pltpu.HBM)
+
+
 def field_call(spectral, shifts, colour, pressure, source):
-    dft_pair, twiddle, order = tables()
     vmem = pl.BlockSpec(memory_space=pltpu.VMEM)
     hbm = pl.BlockSpec(memory_space=pltpu.HBM)
     block = (DEPTH, ITEMS, WIDTH)
@@ -531,7 +616,7 @@
     return pl.pallas_call(
         field_kernel,
         out_shape=[jax.ShapeDtypeStruct(block, F32)] * 2,
-        in_specs=[hbm, vmem] + [hbm] * 6,
+        in_specs=[hbm] * 8,
         out_specs=[vmem, vmem],
         scratch_shapes=[
             pltpu.VMEM((GX, 2, 4, 8, WIDTH), F32),
@@ -545,20 +630,27 @@
             pltpu.VMEM((2, 512, WIDTH), BF16),
             pltpu.VMEM((2, GX, WIDTH), F32),
             pltpu.VMEM((WIDTH, WIDTH), BF16),
-            dma((GX,)), dma((GX,)), dma((GX,)), dma((GX,)), dma((7,)),
+            dma((GX,)), dma((GX,)), dma((GX,)), dma((GX,)), dma((8,)),
             field, field, pltpu.VMEM((ITEMS, WIDTH), jnp.int32),
+            pltpu.VMEM((ITEMS, DEPTH), jnp.int32),
         ]
         + [field] * 12
         + [columns, columns, rows, rows] * 3
-        + [board] * 8
+        + [board] * 4
+        + [
+            pltpu.VMEM((24 * GZ, 128), F32),
+            pltpu.VMEM((24 * GZ, 128), F32),
+            pltpu.VMEM((6, GZ, 128), F32),
+            pltpu.VMEM((2, ITEMS, WIDTH), F32),
+            pltpu.VMEM((GZ, ITEMS, WIDTH), F32),
+        ]
         + [dma((3, 4)), dma((3, 4)), dma((4, GZ)), dma((4, GZ))],
         compiler_params=pltpu.CompilerParams(
             collective_id=0, has_side_effects=True, vmem_limit_bytes=32 << 20
         ),
         name="field",
     )(
-        spectral, shifts.T, jnp.asarray(dft_pair), jnp.asarray(twiddle), jnp.asarray(order),
-        pressure, source, colour,
+        *map(pin, (spectral, shifts.T, *map(jnp.asarray, tables()), pressure, source, colour))
     )
 
 

time: 85 us -> 69.8 us (0.82); the launches traced: 83.8 us -> 69.7 us
  Pallas kernels: 74.8 us -> 67.7 us
  local copies, waits for them, and re-layouts: 8.39 us -> 1.41 us
    pallas_call x1, Pallas kernels: 74.8 us -> 67.7 us  [field_call(): pl.pallas_call(field_kernel, out_shape=[jax.ShapeDtypeStruct(block, F32)]...]
    unnamed x18 -> x2, local copies, waits for them, and re-layouts: 8.39 us -> 1.41 us
where the time goes in v3:
time: 69.8 us; the launch traced here: 69.7 us
  Pallas kernels  67.7 us (97%)
  local copies, waits for them, and re-layouts  1.41 us (2%)
    pallas_call x1, Pallas kernels, field_call(): pl.pallas_call(field_kernel, out_shape=[jax.ShapeDtypeStruct(block, F32)]...  67.7 us
    unnamed x2, local copies, waits for them, and re-layouts  1.41 us

profile of v3, /device:TPU:1, one launch (start us, length us, event | category | flops | bytes accessed | tf_op | source)
XLA Modules:
  0.0 69.7 jit_solution(18309131123407169233)
XLA Ops:
  0.6 67.7 %field.1 = (f32[32,8,256]{2,1,0:T(8,128)S(1)}, f32[32,8,256]{2,1,0:T(8,128)S(1)}) custom-call(f32[2,32,8,256]{3,2,1,0:T(8,128)} %spec.1, s32[8,32]{1,0:T(8,128)} %bitcast.1, bf16[2,512,256]{2,1,0:T(8,128)(2,1)} %constant.6.clone.dft_hbm, f32[2,8,256]{2,1,0:T(8,128)} %constant.7.clone.twiddle_hbm, bf16[256,256]{1,0:T(8,128)(2,1)} %constant.8.clone.order_hbm, ...), custom_call_target="tpu_custom_call" | custom-call | tf_op jit(solution)/shard_map/field/pallas_call | solution.py:616
  68.3 0.7 %copy.12 = f32[32,8,256]{2,1,0:T(8,128)} copy(f32[32,8,256]{2,1,0:T(8,128)S(1)} %get-tuple-element.4) | data formatting | bytes 524288
  69.0 0.7 %copy.13 = f32[32,8,256]{2,1,0:T(8,128)} copy(f32[32,8,256]{2,1,0:T(8,128)S(1)} %get-tuple-element.5) | data formatting | bytes 524288

commit v4 on v3

--- a/solution.py
+++ b/solution.py
@@ -21,6 +21,8 @@
 ITEMS = 8
 WIDTH = 256
 ROWS = 32
+FAR_FIRST = (9, 7, 11, 5, 13, 3, 8, 15, 1, 10, 6, 12, 4, 14, 2)
+ROUND_FIRST = (8, 6, 10, 4, 12, 2, 14)
 F32 = jnp.float32
 BF16 = jnp.bfloat16
 
@@ -254,12 +256,9 @@
     def greet_all():
         barrier = pltpu.get_barrier_semaphore()
 
-        def greet(i, carry):
+        for i in FAR_FIRST:
             peer = lax.rem(gz + i, GZ)
             pl.semaphore_signal(barrier, inc=1, device_id={"gz": peer}, device_id_type=MESH)
-            return carry
-
-        lax.fori_loop(1, GZ, greet, 0)
         for i in range(1, GX):
             peer = lax.rem(gx + i, GX)
             pl.semaphore_signal(barrier, inc=1, device_id={"gx": peer}, device_id_type=MESH)
@@ -397,36 +396,47 @@
             [ref[pl.ds(8 * h + kind, 8, stride=16), :] for h in range(2)], axis=1
         )
 
-    def everyone(src, dst, phase, size):
+    row = lax.div(gz, 2)
+
+    def everyone(src, dst, phase, size, offsets, to_owner):
         def tile(index):
             return pl.ds(pl.multiple_of(size * index, 8), size)
 
-        def copy(peer, slot):
+        def copy(peer, slot, first, then):
             return pltpu.make_async_remote_copy(
-                src_ref=src.at[tile(peer)], dst_ref=dst.at[tile(slot)],
+                src_ref=src.at[tile(first)], dst_ref=dst.at[tile(then)],
                 send_sem=gz_send.at[phase, peer], recv_sem=gz_recv.at[phase, slot],
                 device_id={"gz": peer}, device_id_type=MESH,
             )
 
-        def start(i, carry):
+        def outward(i):
             peer = lax.rem(gz + i, GZ)
-            copy(peer, gz).start()
-            return carry
-
-        def finish(i, carry):
+            if to_owner:
+                return copy(peer, gz, lax.div(peer, 2), gz)
+            return copy(peer, gz, peer, row)
+
+        def inward(i):
             peer = lax.rem(gz + GZ - i, GZ)
-            copy(peer, peer).wait_recv()
-            return carry
-
-        def drain(i, carry):
-            peer = lax.rem(gz + i, GZ)
-            copy(peer, gz).wait_send()
-            return carry
-
-        lax.fori_loop(1, GZ, start, 0)
-        dst[tile(gz), :] = src[tile(gz), :]
-        drains.append(lambda: lax.fori_loop(1, GZ, drain, 0))
-        return lambda: lax.fori_loop(1, GZ, finish, 0)
+            if to_owner:
+                return copy(peer, peer, 0, peer)
+            return copy(peer, peer, 0, lax.div(peer, 2))
+
+        def finish():
+            for i in offsets:
+                inward(i).wait_recv()
+
+        def drain():
+            for i in offsets:
+                outward(i).wait_send()
+
+        for i in offsets:
+            outward(i).start()
+        if to_owner:
+            dst[tile(gz), :] = src[tile(row), :]
+        else:
+            dst[tile(row), :] = src[tile(gz), :]
+        drains.append(drain)
+        return finish
 
     put(msg, 0, dd[0])
     put(msg, 1, dd[DEPTH - 1])
@@ -436,14 +446,20 @@
     put(msg, 5, ff[0])
     put(msg, 6, ff[DEPTH - 1])
     put(msg, 7, ff[0])
-    everyone(msg, got, 0, 8)()
+    everyone(msg, got, 0, 16, FAR_FIRST, True)()
 
     def kind(ref, k):
-        return ref[pl.ds(k, GZ, stride=8), :]
+        return jnp.concatenate(
+            [ref[pl.ds(8 * h + k, GZ, stride=16), :] for h in range(2)], axis=1
+        )
+
+    def spread(ref, size, k, value):
+        for h in range(2):
+            ref[pl.ds(size * h + k, GZ, stride=2 * size), :] = value[:, 128 * h:128 * h + 128]
 
     d0, d1, c, p0, p1 = (kind(got, k) for k in range(5))
     f0, f1 = kind(got, 5), kind(got, 6)
-    segment = lax.broadcasted_iota(jnp.int32, (GZ, 128), 0)
+    segment = lax.broadcasted_iota(jnp.int32, (GZ, WIDTH), 0)
     w = jnp.where(segment < GZ - 1, VERT * harmonic(p1, pltpu.roll(p0, GZ - 1, 0)), 0.0)
     last_inv = 1.0 / (d1 + c + w)
     last_l, last_r = c * last_inv, w * last_inv
@@ -467,13 +483,11 @@
             a, b = alpha * up(a, step), beta * down(b, step)
     first = f / e
     ans[...] = jnp.zeros_like(ans)
-    ans[pl.ds(0, GZ, stride=8), :] = first
-    ans[pl.ds(1, GZ, stride=8), :] = (
-        f1 * last_inv + last_l * first + last_r * down(first, 1)
-    )
-    wait_sol = everyone(ans, sol, 1, 8)
-
-    links = [jnp.zeros((1, 128), F32)] * 2
+    spread(ans, 8, 0, first)
+    spread(ans, 8, 1, f1 * last_inv + last_l * first + last_r * down(first, 1))
+    wait_sol = everyone(ans, sol, 1, 16, ROUND_FIRST, False)
+
+    links = [jnp.zeros((1, WIDTH), F32)] * 2
     for i in range(GZ):
         j = GZ - 1 - i
         eb, et = links
@@ -494,7 +508,7 @@
             upsilon = w[j - 1:j] / (high + w[j - 1:j])
             chain[4, pl.ds(j - 1, 1), :] = upsilon
         links = [tau * low, upsilon * high]
-    chain[4, pl.ds(GZ - 1, 1), :] = jnp.zeros((1, 128), F32)
+    chain[4, pl.ds(GZ - 1, 1), :] = jnp.zeros((1, WIDTH), F32)
     tau, upsilon = chain[1], chain[4]
     climb = up(tau * chain[0], 1)
     descend = upsilon * down(chain[3], 1)
@@ -504,10 +518,10 @@
         from_above.append(descend * down(from_above[-1], 1))
     gains[...] = jnp.zeros_like(gains)
     for k in range(1, GZ):
-        gains[pl.ds(k, GZ, stride=24), :] = from_below[k] + from_above[GZ - k]
-    gains[pl.ds(GZ, GZ, stride=24), :] = chain[2]
-    gains[pl.ds(GZ + 1, GZ, stride=24), :] = chain[5]
-    wait_gains = everyone(gains, taken, 2, 24)
+        spread(gains, 24, k, from_below[k] + from_above[GZ - k])
+    spread(gains, 24, GZ, chain[2])
+    spread(gains, 24, GZ + 1, chain[5])
+    wait_gains = everyone(gains, taken, 2, 48, ROUND_FIRST, False)
     wait_sol()
 
     def substitute(first, last, merge):
@@ -570,21 +584,15 @@
             device_id={"gz": peer}, device_id_type=MESH,
         )
 
-    def start_cast(i, carry):
+    def drain_cast():
+        for i in FAR_FIRST:
+            cast(i).wait_send()
+
+    for i in FAR_FIRST:
         cast(i).start()
-        return carry
-
-    def drain_cast(i, carry):
-        cast(i).wait_send()
-        return carry
-
-    def wait_heard(i, carry):
+    drains.append(drain_cast)
+    for i in FAR_FIRST:
         heard(i).wait_recv()
-        return carry
-
-    lax.fori_loop(1, GZ, start_cast, 0)
-    drains.append(lambda: lax.fori_loop(1, GZ, drain_cast, 0))
-    lax.fori_loop(1, GZ, wait_heard, 0)
     for i in range(1, GZ):
         part = gain(i) * others[lax.rem(gz + GZ - i, GZ)]
         f0 = f0 + jnp.where(gz >= i, part, 0.0)
@@ -610,6 +618,7 @@
     block = (DEPTH, ITEMS, WIDTH)
     field = pltpu.VMEM(block, F32)
     board = pltpu.VMEM((8 * GZ, 128), F32)
+    pair_board = pltpu.VMEM((16 * GZ, 128), F32)
     columns = pltpu.VMEM((2, ITEMS, 128), F32)
     rows = pltpu.VMEM((2, DEPTH, WIDTH), F32)
     dma = pltpu.SemaphoreType.DMA
@@ -636,11 +645,11 @@
         ]
         + [field] * 12
         + [columns, columns, rows, rows] * 3
-        + [board] * 4
+        + [board, pair_board, pair_board, board]
         + [
+            pltpu.VMEM((48 * GZ, 128), F32),
             pltpu.VMEM((24 * GZ, 128), F32),
-            pltpu.VMEM((24 * GZ, 128), F32),
-            pltpu.VMEM((6, GZ, 128), F32),
+            pltpu.VMEM((6, GZ, WIDTH), F32),
             pltpu.VMEM((2, ITEMS, WIDTH), F32),
             pltpu.VMEM((GZ, ITEMS, WIDTH), F32),
         ]

time: 69.8 us -> 65.9 us (0.944)
  Pallas kernels: 67.7 us -> 63.4 us
    pallas_call x1, Pallas kernels: 67.7 us -> 63.4 us  [field_call(): pl.pallas_call(field_kernel, out_shape=[jax.ShapeDtypeStruct(block, F32)]...]
where the time goes in v4:
time: 65.9 us; the launch traced here: 65.5 us
  Pallas kernels  63.4 us (96%)
  local copies, waits for them, and re-layouts  1.41 us (2%)
    pallas_call x1, Pallas kernels, field_call(): pl.pallas_call(field_kernel, out_shape=[jax.ShapeDtypeStruct(block, F32)]...  63.4 us
    unnamed x2, local copies, waits for them, and re-layouts  1.41 us

profile of v4, /device:TPU:1, one launch (start us, length us, event | category | flops | bytes accessed | tf_op | source)
XLA Modules:
  0.0 65.5 jit_solution(18125857309064804837)
XLA Ops:
  0.6 63.4 %field.1 = (f32[32,8,256]{2,1,0:T(8,128)S(1)}, f32[32,8,256]{2,1,0:T(8,128)S(1)}) custom-call(f32[2,32,8,256]{3,2,1,0:T(8,128)} %spec.1, s32[8,32]{1,0:T(8,128)} %bitcast.1, bf16[2,512,256]{2,1,0:T(8,128)(2,1)} %constant.6.clone.dft_hbm, f32[2,8,256]{2,1,0:T(8,128)} %constant.7.clone.twiddle_hbm, bf16[256,256]{1,0:T(8,128)(2,1)} %constant.8.clone.order_hbm, ...), custom_call_target="tpu_custom_call" | custom-call | tf_op jit(solution)/shard_map/field/pallas_call | solution.py:625
  64.1 0.7 %copy.12 = f32[32,8,256]{2,1,0:T(8,128)} copy(f32[32,8,256]{2,1,0:T(8,128)S(1)} %get-tuple-element.4) | data formatting | bytes 524288
  64.8 0.7 %copy.13 = f32[32,8,256]{2,1,0:T(8,128)} copy(f32[32,8,256]{2,1,0:T(8,128)S(1)} %get-tuple-element.5) | data formatting | bytes 524288

commit v5 on v4

--- a/solution.py
+++ b/solution.py
@@ -22,6 +22,7 @@
 WIDTH = 256
 ROWS = 32
 FAR_FIRST = (9, 7, 11, 5, 13, 3, 8, 15, 1, 10, 6, 12, 4, 14, 2)
+RELAYS = 4
 ROUND_FIRST = (8, 6, 10, 4, 12, 2, 14)
 F32 = jnp.float32
 BF16 = jnp.bfloat16
@@ -239,7 +240,7 @@
         perm, half, ww, we, ws, wn, dd, ff, cc, ll, rr, iv,
         xs0, xh0, ys0, yh0, xs1, xh1, ys1, yh1, xs2, xh2, ys2, yh2,
         msg, got, ans, sol, gains, taken, chain, sums, others,
-        halo_send, halo_recv, gz_send, gz_recv,
+        halo_send, halo_recv, gz_send, gz_recv, relay,
     ) = scratch
     gx = lax.axis_index("gx")
     gy = lax.axis_index("gy")
@@ -247,6 +248,8 @@
     left, right = lax.rem(gx + GX - 1, GX), lax.rem(gx + 1, GX)
     south, north = lax.rem(gy + GY - 1, GY), lax.rem(gy + 1, GY)
     drains = []
+    twin = gz + 1 - 2 * lax.rem(gz, 2)
+    round_neighbours = (lax.rem(gz + 2, GZ), lax.rem(gz + GZ - 2, GZ))
 
     pressure_copy = pltpu.make_async_copy(pressure_hbm, pressure, local.at[4])
     source_copy = pltpu.make_async_copy(source_hbm, source, local.at[5])
@@ -256,8 +259,7 @@
     def greet_all():
         barrier = pltpu.get_barrier_semaphore()
 
-        for i in FAR_FIRST:
-            peer = lax.rem(gz + i, GZ)
+        for peer in (twin, *round_neighbours):
             pl.semaphore_signal(barrier, inc=1, device_id={"gz": peer}, device_id_type=MESH)
         for i in range(1, GX):
             peer = lax.rem(gx + i, GX)
@@ -268,7 +270,7 @@
         pressure_copy.start()
         source_copy.start()
         colour_copy.start()
-        pl.semaphore_wait(barrier, GX - 1 + GZ - 1 + 2)
+        pl.semaphore_wait(barrier, GX - 1 + 3 + 2)
 
     lane1 = lax.broadcasted_iota(jnp.int32, (8, 128), 1)
     lane = lax.broadcasted_iota(jnp.int32, (8, WIDTH), 1)
@@ -329,6 +331,12 @@
         pack(pressure, xs0, ys0)
         arrived.append(halo(0, xs0, xh0, ys0, yh0))
         shifts_copy.wait()
+        for turn in range(RELAYS):
+            for peer in round_neighbours:
+                pl.semaphore_signal(
+                    relay.at[turn], inc=1, device_id={"gz": peer}, device_id_type=MESH
+                )
+            pl.semaphore_wait(relay.at[turn], 2)
 
     drains.append(
         spectral_part(
@@ -653,7 +661,8 @@
             pltpu.VMEM((2, ITEMS, WIDTH), F32),
             pltpu.VMEM((GZ, ITEMS, WIDTH), F32),
         ]
-        + [dma((3, 4)), dma((3, 4)), dma((4, GZ)), dma((4, GZ))],
+        + [dma((3, 4)), dma((3, 4)), dma((4, GZ)), dma((4, GZ))]
+        + [pltpu.SemaphoreType.REGULAR((RELAYS,))],
         compiler_params=pltpu.CompilerParams(
             collective_id=0, has_side_effects=True, vmem_limit_bytes=32 << 20
         ),

time: 65.9 us -> 64 us (0.971)
  Pallas kernels: 63.4 us -> 61.8 us
    pallas_call x1, Pallas kernels: 63.4 us -> 61.8 us  [field_call(): pl.pallas_call(field_kernel, out_shape=[jax.ShapeDtypeStruct(block, F32)]...]
where the time goes in v5:
time: 64 us; the launch traced here: 63.9 us
  Pallas kernels  61.8 us (97%)
  local copies, waits for them, and re-layouts  1.41 us (2%)
  between operations  0.64 us (1%)
    pallas_call x1, Pallas kernels, field_call(): pl.pallas_call(field_kernel, out_shape=[jax.ShapeDtypeStruct(block, F32)]...  61.8 us
    unnamed x2, local copies, waits for them, and re-layouts  1.41 us

profile of v5, /device:TPU:1, one launch (start us, length us, event | category | flops | bytes accessed | tf_op | source)
XLA Modules:
  0.0 63.9 jit_solution(16075321440752969481)
XLA Ops:
  0.6 61.8 %field.1 = (f32[32,8,256]{2,1,0:T(8,128)S(1)}, f32[32,8,256]{2,1,0:T(8,128)S(1)}) custom-call(f32[2,32,8,256]{3,2,1,0:T(8,128)} %spec.1, s32[8,32]{1,0:T(8,128)} %bitcast.1, bf16[2,512,256]{2,1,0:T(8,128)(2,1)} %constant.6.clone.dft_hbm, f32[2,8,256]{2,1,0:T(8,128)} %constant.7.clone.twiddle_hbm, bf16[256,256]{1,0:T(8,128)(2,1)} %constant.8.clone.order_hbm, ...), custom_call_target="tpu_custom_call" | custom-call | tf_op jit(solution)/shard_map/field/pallas_call | solution.py:633
  62.4 0.7 %copy.12 = f32[32,8,256]{2,1,0:T(8,128)} copy(f32[32,8,256]{2,1,0:T(8,128)S(1)} %get-tuple-element.4) | data formatting | bytes 524288
  63.1 0.7 %copy.13 = f32[32,8,256]{2,1,0:T(8,128)} copy(f32[32,8,256]{2,1,0:T(8,128)S(1)} %get-tuple-element.5) | data formatting | bytes 524288

commit v6 on v5

--- a/solution.py
+++ b/solution.py
@@ -89,7 +89,7 @@
 def spectral_part(
     spec, shifts, dft_hbm, twiddle_hbm, order_hbm, out,
     xb, trig, lhs_hi, lhs_lo, zb, wb_hi, wb_lo, sb, dft, twiddle, order,
-    send1, recv1, send2, recv2, local, greet_all, meanwhile,
+    send1, recv1, send2, recv2, local, greet_all, meanwhile, spill,
 ):
     me = lax.axis_index("gx")
 
@@ -199,6 +199,7 @@
             device_id={"gx": who}, device_id_type=MESH,
         )
 
+    spill()
     for i in range(1, GX):
         peer = lax.rem(me + i, GX)
         second(peer, me, peer).start()
@@ -238,9 +239,9 @@
         send1, recv1, send2, recv2, local,
         pressure, source, colour, shifts,
         perm, half, ww, we, ws, wn, dd, ff, cc, ll, rr, iv,
-        xs0, xh0, ys0, yh0, xs1, xh1, ys1, yh1, xs2, xh2, ys2, yh2,
+        xs0, xh0, ys0, yh0, xspill, xgot, yspill, ygot, xs2, xh2, ys2, yh2,
         msg, got, ans, sol, gains, taken, chain, sums, others,
-        halo_send, halo_recv, gz_send, gz_recv, relay,
+        halo_send, halo_recv, gz_send, gz_recv, relay, spill_send, spill_recv,
     ) = scratch
     gx = lax.axis_index("gx")
     gy = lax.axis_index("gy")
@@ -337,12 +338,94 @@
                     relay.at[turn], inc=1, device_id={"gz": peer}, device_id_type=MESH
                 )
             pl.semaphore_wait(relay.at[turn], 2)
+        for who in (south, north):
+            pl.semaphore_signal(
+                relay.at[RELAYS], inc=1, device_id={"gy": who}, device_id_type=MESH
+            )
+        pl.semaphore_wait(relay.at[RELAYS], 2)
+
+    def column_copy(peer, slot):
+        return pltpu.make_async_remote_copy(
+            src_ref=xspill.at[peer], dst_ref=xgot.at[slot],
+            send_sem=spill_send.at[2, peer], recv_sem=spill_recv.at[2, slot],
+            device_id={"gx": peer}, device_id_type=MESH,
+        )
+
+    rims = ((1, south, gy > 0, gy < GY - 1), (0, north, gy < GY - 1, gy > 0))
+
+    def rim_copy(k, peer, slot):
+        there, who, _, _ = rims[k]
+        return pltpu.make_async_remote_copy(
+            src_ref=yspill.at[k, peer], dst_ref=ygot.at[there, slot],
+            send_sem=spill_send.at[k, peer], recv_sem=spill_recv.at[k, slot],
+            device_id={"gx": peer, "gy": who}, device_id_type=MESH,
+        )
+
+    def spill():
+        for k, y in ((0, 0), (1, 7)):
+            for e in range(GX):
+                for z in range(4):
+                    edge = sb[e, z][y:y + 1, :]
+                    for h in range(2):
+                        yspill[k, e, pl.ds(2 * z + h, 1), :] = edge[:, 128 * h:128 * h + 128]
+            yspill[k] = jnp.exp(yspill[k])
+            there, _, sends, receives = rims[k]
+
+            def start(k=k):
+                for i in range(GX):
+                    rim_copy(k, lax.rem(gx + i, GX), gx).start()
+
+            def drain(k=k):
+                for i in range(GX):
+                    rim_copy(k, lax.rem(gx + i, GX), gx).wait_send()
+
+            def blank(there=there):
+                ygot[there] = jnp.zeros(ygot.shape[1:], F32)
+
+            pl.when(sends)(start)
+            pl.when(jnp.logical_not(receives))(blank)
+            drains.append(lambda sends=sends, drain=drain: pl.when(sends)(drain))
+        for e in range(GX):
+            tile = jnp.zeros((8, 128), F32)
+            for z in range(4):
+                if e > 0:
+                    tile = jnp.where(lane1 == 2 * z, sb[e - 1, z][:, 255:256], tile)
+                if e < GX - 1:
+                    tile = jnp.where(lane1 == 2 * z + 1, sb[e + 1, z][:, 0:1], tile)
+            tile = jnp.exp(tile)
+            if e == 0:
+                tile = jnp.where(lane1 % 2 == 0, 0.0, tile)
+            if e == GX - 1:
+                tile = jnp.where(lane1 % 2 == 1, 0.0, tile)
+            xspill[e] = tile
+        for i in range(1, GX):
+            column_copy(lax.rem(gx + i, GX), gx).start()
+        xgot[gx] = xspill[gx]
+
+        def drain_columns():
+            for i in range(1, GX):
+                column_copy(lax.rem(gx + i, GX), gx).wait_send()
+
+        drains.append(drain_columns)
+
+    def wait_spill():
+        for i in range(1, GX):
+            peer = lax.rem(gx + GX - i, GX)
+            column_copy(peer, peer).wait_recv()
+        for k in range(2):
+
+            def wait(k=k):
+                for i in range(GX):
+                    peer = lax.rem(gx + GX - i, GX)
+                    rim_copy(k, peer, peer).wait_recv()
+
+            pl.when(rims[k][3])(wait)
 
     drains.append(
         spectral_part(
             spec, shifts, dft_hbm, twiddle_hbm, order_hbm, log_perm,
             xb, trig, lhs_hi, lhs_lo, zb, wb_hi, wb_lo, sb, dft, twiddle, order,
-            send1, recv1, send2, recv2, local, greet_all, meanwhile,
+            send1, recv1, send2, recv2, local, greet_all, meanwhile, spill,
         )
     )
 
@@ -351,12 +434,10 @@
         return carry
 
     lax.fori_loop(0, DEPTH, make_perm, 0, unroll=4)
-    pack(perm, xs1, ys1)
-    wait_perm = halo(1, xs1, xh1, ys1, yh1)
     source_copy.wait()
     colour_copy.wait()
     arrived[0]()
-    wait_perm()
+    wait_spill()
 
     def beside(value, west, east, lower, upper):
         vw = jnp.where(lane == 0, west, pltpu.roll(value, 1, 1))
@@ -365,6 +446,18 @@
         vn = jnp.where(sub == 7, upper, pltpu.roll(value, 7, 0))
         return vw, ve, vs, vn
 
+    def spilled(z):
+        owner, place = z // 4, 2 * (z % 4)
+        west = xgot[owner][:, place:place + 1]
+        east = xgot[owner][:, place + 1:place + 2]
+        lower, upper = (
+            jnp.concatenate(
+                [ygot[k, owner, pl.ds(place + h, 1), :] for h in range(2)], axis=1
+            )
+            for k in range(2)
+        )
+        return west, east, lower, upper
+
     def edges(z, xh, yh):
         west = xh[0][:, z:z + 1]
         east = xh[1][:, z:z + 1]
@@ -374,7 +467,7 @@
 
     for z in range(DEPTH):
         p = perm[z]
-        pw, pe, ps, pn = beside(p, *edges(z, xh1, yh1))
+        pw, pe, ps, pn = beside(p, *spilled(z))
         aw, ae, as_, an = harmonic(p, pw), harmonic(p, pe), harmonic(p, ps), harmonic(p, pn)
         ww[z], we[z], ws[z], wn[z] = aw, ae, as_, an
         dd[z] = STORE + aw + ae + as_ + an
@@ -629,6 +722,7 @@
     pair_board = pltpu.VMEM((16 * GZ, 128), F32)
     columns = pltpu.VMEM((2, ITEMS, 128), F32)
     rows = pltpu.VMEM((2, DEPTH, WIDTH), F32)
+    tiles = pltpu.VMEM((GX, 8, 128), F32)
     dma = pltpu.SemaphoreType.DMA
     return pl.pallas_call(
         field_kernel,
@@ -652,7 +746,9 @@
             pltpu.VMEM((ITEMS, DEPTH), jnp.int32),
         ]
         + [field] * 12
-        + [columns, columns, rows, rows] * 3
+        + [columns, columns, rows, rows]
+        + [tiles, tiles, pltpu.VMEM((2, GX, 8, 128), F32), pltpu.VMEM((2, GX, 8, 128), F32)]
+        + [columns, columns, rows, rows]
         + [board, pair_board, pair_board, board]
         + [
             pltpu.VMEM((48 * GZ, 128), F32),
@@ -662,7 +758,7 @@
             pltpu.VMEM((GZ, ITEMS, WIDTH), F32),
         ]
         + [dma((3, 4)), dma((3, 4)), dma((4, GZ)), dma((4, GZ))]
-        + [pltpu.SemaphoreType.REGULAR((RELAYS,))],
+        + [pltpu.SemaphoreType.REGULAR((RELAYS + 1,)), dma((3, GX)), dma((3, GX))],
         compiler_params=pltpu.CompilerParams(
             collective_id=0, has_side_effects=True, vmem_limit_bytes=32 << 20
         ),

time: 64 us -> 62.8 us (0.981)
  Pallas kernels: 61.8 us -> 60.1 us
    pallas_call x1, Pallas kernels: 61.8 us -> 60.1 us  [field_call(): pl.pallas_call(field_kernel, out_shape=[jax.ShapeDtypeStruct(block, F32)]...]
where the time goes in v6:
time: 62.8 us; the launch traced here: 62.1 us
  Pallas kernels  60.1 us (96%)
  local copies, waits for them, and re-layouts  1.41 us (2%)
  between operations  0.64 us (1%)
    pallas_call x1, Pallas kernels, field_call(): pl.pallas_call(field_kernel, out_shape=[jax.ShapeDtypeStruct(block, F32)]...  60.1 us
    unnamed x2, local copies, waits for them, and re-layouts  1.41 us

profile of v6, /device:TPU:1, one launch (start us, length us, event | category | flops | bytes accessed | tf_op | source)
XLA Modules:
  0.0 62.1 jit_solution(11681568949399519335)
XLA Ops:
  0.6 60.1 %field.1 = (f32[32,8,256]{2,1,0:T(8,128)S(1)}, f32[32,8,256]{2,1,0:T(8,128)S(1)}) custom-call(f32[2,32,8,256]{3,2,1,0:T(8,128)} %spec.1, s32[8,32]{1,0:T(8,128)} %bitcast.1, bf16[2,512,256]{2,1,0:T(8,128)(2,1)} %constant.6.clone.dft_hbm, f32[2,8,256]{2,1,0:T(8,128)} %constant.7.clone.twiddle_hbm, bf16[256,256]{1,0:T(8,128)(2,1)} %constant.8.clone.order_hbm, ...), custom_call_target="tpu_custom_call" | custom-call | tf_op jit(solution)/shard_map/field/pallas_call | solution.py:727
  60.7 0.7 %copy.12 = f32[32,8,256]{2,1,0:T(8,128)} copy(f32[32,8,256]{2,1,0:T(8,128)S(1)} %get-tuple-element.4) | data formatting | bytes 524288
  61.4 0.7 %copy.13 = f32[32,8,256]{2,1,0:T(8,128)} copy(f32[32,8,256]{2,1,0:T(8,128)S(1)} %get-tuple-element.5) | data formatting | bytes 524288

commit v7 on v6

--- a/solution.py
+++ b/solution.py
@@ -232,8 +232,9 @@
 
 def field_kernel(
     spec, shifts_hbm, dft_hbm, twiddle_hbm, order_hbm, pressure_hbm, source_hbm, colour_hbm,
-    log_perm, out, *scratch,
+    both, *scratch,
 ):
+    log_perm, out = both.at[0], both.at[1]
     (
         xb, trig, lhs_hi, lhs_lo, zb, wb_hi, wb_lo, sb, dft, twiddle, order,
         send1, recv1, send2, recv2, local,
@@ -726,9 +727,9 @@
     dma = pltpu.SemaphoreType.DMA
     return pl.pallas_call(
         field_kernel,
-        out_shape=[jax.ShapeDtypeStruct(block, F32)] * 2,
+        out_shape=jax.ShapeDtypeStruct((2, *block), F32),
         in_specs=[hbm] * 8,
-        out_specs=[vmem, vmem],
+        out_specs=vmem,
         scratch_shapes=[
             pltpu.VMEM((GX, 2, 4, 8, WIDTH), F32),
             pltpu.VMEM((2, GX, ROWS, WIDTH), F32),
@@ -769,8 +770,8 @@
 
 
 def body(spectral, shifts, colour, pressure, source):
-    log_perm, smoothed = field_call(spectral, shifts, colour, pressure, source)
-    return (log_perm, smoothed)
+    both = field_call(spectral, shifts, colour, pressure, source)
+    return (both[0], both[1])
 
 
 def solution(mesh):

time: 62.8 us -> 62.3 us (level)
    unnamed x2 -> x0, local copies, waits for them, and re-layouts: 1.41 us -> none
    squeeze x0 -> x1, local copies, waits for them, and re-layouts: none -> 0.82 us  [body(): return (both[0], both[1])]
where the time goes in v7:
time: 62.3 us; the launch traced here: 61.6 us
  Pallas kernels  60.2 us (97%)
  local copies, waits for them, and re-layouts  0.82 us (1%)
  between operations  0.64 us (1%)
    pallas_call x1, Pallas kernels, field_call(): pl.pallas_call(field_kernel, out_shape=jax.ShapeDtypeStruct((2, *block),...  60.2 us

profile of v7, /device:TPU:1, one launch (start us, length us, event | category | flops | bytes accessed | tf_op | source)
XLA Modules:
  0.0 61.6 jit_solution(6946635570777667142)
XLA Ops:
  0.6 60.2 %field.1 = f32[2,32,8,256]{3,2,1,0:T(8,128)S(1)} custom-call(f32[2,32,8,256]{3,2,1,0:T(8,128)} %spec.1, s32[8,32]{1,0:T(8,128)} %bitcast.5, bf16[2,512,256]{2,1,0:T(8,128)(2,1)} %constant.6.clone.dft_hbm, f32[2,8,256]{2,1,0:T(8,128)} %constant.7.clone.twiddle_hbm, bf16[256,256]{1,0:T(8,128)(2,1)} %constant.8.clone.order_hbm, f32[32,8,256]{2,1,0:T(8,128)} %pressure_hbm.1, ...), custom_call_target="tpu_custom_call" | custom-call | tf_op jit(solution)/shard_map/field/pallas_call | solution.py:728
  60.8 0.8 %slice_bitcast_fusion = (f32[32,8,256]{2,1,0:T(8,128)}, f32[32,8,256]{2,1,0:T(8,128)}) fusion(f32[2,32,8,256]{3,2,1,0:T(8,128)S(1)} %field.1), kind=kLoop, calls=%fused_computation | loop fusion | bytes 1048576 | tf_op jit(solution)/shard_map/squeeze | solution.py:774
